TPU v7x, 32 devices: a whole 2x2x4 slice. The times are simulated.
32 devices in a mesh: dp: 4 (over z), row: 4 (over x, core), col: 2 (over y).
Axes of the slice: x: 2, y: 2, z: 4, core: 2. Of those that a mesh axis runs over, the one named last changes fastest.
Arguments:
- tokens: bfloat16 [16384, 1024], P(('dp', 'col'), 'row'), may hold values from -11 to 11
- segments: int32 [32, 512], P(('dp', 'row')), may hold values from 0 to 3, never falling along the last dimension, each value on 1 to 256 neighbouring positions
- cotangent: bfloat16 [16384, 1024], P(('dp', 'col'), 'row'), may hold values from -6 to 6
- in_proj: float32 [1024, 3, 1024], P('row', None, 'col'), may hold values from -0.1875 to 0.1875
- entry_bias: float32 [2, 1024], P(None, 'col'), may hold values from -0.3 to 0.3
- out_proj: float32 [1024, 1024], P('col', 'row'), may hold values from -2 to 2
- up_proj: float32 [1024, 4096], P('row', 'col'), may hold values from -0.1875 to 0.1875
- hidden_bias: float32 [4096], P('col'), may hold values from -3 to 3
- down_proj: float32 [4096, 1024], P('col', 'row'), may hold values from -0.09375 to 0.09375
- norm_gains: float32 [2, 1024], P(None, 'row'), may hold values from 0.5 to 1.5
- row_biases: float32 [4, 1024], P(None, 'row'), may hold values from -3 to 3
- moments_in: float32 [2, 1024, 3, 1024], P(None, 'row', None, 'col'), as said below
- moments_entry: float32 [2, 2, 1024], P(None, None, 'col'), as said below
- moments_out: float32 [2, 1024, 1024], P(None, 'col', 'row'), as said below
- moments_up: float32 [2, 1024, 4096], P(None, 'row', 'col'), as said below
- moments_hidden: float32 [2, 4096], P(None, 'col'), as said below
- moments_down: float32 [2, 4096, 1024], P(None, 'col', 'row'), as said below
- moments_gains: float32 [2, 2, 1024], P(None, None, 'row'), as said below
- moments_biases: float32 [2, 4, 1024], P(None, None, 'row'), as said below
Outputs:
- layer_out: bfloat16 [16384, 1024], P(('dp', 'col'), 'row')
- input_grad: bfloat16 [16384, 1024], P(('dp', 'col'), 'row')
- grad_in: float32 [1024, 3, 1024], P('row', None, 'col')
- grad_entry: float32 [2, 1024], P(None, 'col')
- grad_out: float32 [1024, 1024], P('col', 'row')
- grad_up: float32 [1024, 4096], P('row', 'col')
- grad_hidden: float32 [4096], P('col')
- grad_down: float32 [4096, 1024], P('col', 'row')
- grad_gains: float32 [2, 1024], P(None, 'row')
- grad_biases: float32 [4, 1024], P(None, 'row')
- update_in: float32 [1024, 3, 1024], P('row', None, 'col')
- update_entry: float32 [2, 1024], P(None, 'col')
- update_out: float32 [1024, 1024], P('col', 'row')
- update_up: float32 [1024, 4096], P('row', 'col')
- update_hidden: float32 [4096], P('col')
- update_down: float32 [4096, 1024], P('col', 'row')
- update_gains: float32 [2, 1024], P(None, 'row')
- update_biases: float32 [4, 1024], P(None, 'row')
- state_in: float32 [2, 1024, 3, 1024], P(None, 'row', None, 'col')
- state_entry: float32 [2, 2, 1024], P(None, None, 'col')
- state_out: float32 [2, 1024, 1024], P(None, 'col', 'row')
- state_up: float32 [2, 1024, 4096], P(None, 'row', 'col')
- state_hidden: float32 [2, 4096], P(None, 'col')
- state_down: float32 [2, 4096, 1024], P(None, 'col', 'row')
- state_gains: float32 [2, 2, 1024], P(None, None, 'row')
- state_biases: float32 [2, 4, 1024], P(None, None, 'row')
Inputs may be any that keep to these rules, and one draw needn't show every extreme that they name: `segments`: each sequence holds at most 4 documents of 1 to 256 tokens, one of exactly 256; numbers never fall along a sequence. `moments_in`: index 0 holds first moments, index 1 positive second moments. `moments_entry`: index 0 holds first moments, index 1 positive second moments. `moments_out`: index 0 holds first moments, index 1 positive second moments. `moments_up`: index 0 holds first moments, index 1 positive second moments. `moments_hidden`: index 0 holds first moments, index 1 positive second moments. `moments_down`: index 0 holds first moments, index 1 positive second moments. `moments_gains`: index 0 holds first moments, index 1 positive second moments. `moments_biases`: index 0 holds first moments, index 1 positive second moments.
All inputs are finite; a program needn't handle non-finite values.
Results may differ from a plain program's by a relative error of at most 0.015.
The roundings to bfloat16 on the way count: a program that leaves them out, or rounds other values in their place, can miss the bound.
Values may be sent and summed in bfloat16 or wider, within the bound.
No kernel may reach another device: no remote copies, remote signals or barrier semaphores. Data moves between devices by JAX's collectives and lax.ppermute only.
A program may use at most 256 MiB of HBM per device.

v0:
```python
import jax
import jax.numpy as jnp
from jax import lax
from jax.sharding import PartitionSpec as P

HD = 64


LN_EPS = 1e-05
BETA_ONE = 0.9
BETA_TWO = 0.999
ADAM_EPS = 1e-08
STEP_COUNT = 2
MASK_FILL = -1e30


def rounded(values):
    return lax.optimization_barrier(values.astype(jnp.bfloat16)).astype(jnp.float32)


def gelu_value(pre_act):
    return pre_act * (0.5 * (1.0 + lax.erf(pre_act * 2.0 ** (-0.5))))


def gelu_slope(pre_act):
    cumul = 0.5 * (1.0 + lax.erf(pre_act * 2.0 ** (-0.5)))
    density = jnp.exp(-0.5 * pre_act * pre_act) * (2.0 * jnp.pi) ** (-0.5)
    return cumul + pre_act * density


def spread_cols(block):
    return lax.all_gather(block, "col", axis=0, tiled=True)


def spread_rows(block):
    return lax.all_gather(block, "row", axis=0, tiled=True)


def row_totals(values):
    return lax.psum(values, "row")


def contract(left_side, right_side, flipped):
    right_dim = (1,) if flipped else (0,)
    return lax.dot_general(
        left_side, right_side, (((1,), right_dim), ((), ())), preferred_element_type=jnp.float32
    )


def outer_sum(left_side, right_side):
    return lax.dot_general(
        left_side, right_side, (((0,), (0,)), ((), ())), preferred_element_type=jnp.float32
    )


def reduce_rows(left_side, right_side, flipped):
    row_count = left_side.shape[0] // lax.axis_size("row")

    def partial_term(begin_row, length):
        return contract(left_side, right_side, flipped)

    return lax.psum_scatter(
        partial_term(jnp.int32(0), row_count * lax.axis_size("row")),
        "row",
        scatter_dimension=0,
        tiled=True,
    )


def reduce_cols(left_side, right_side, flipped):
    row_count = left_side.shape[0] // lax.axis_size("col")

    def partial_term(begin_row, length):
        return contract(left_side, right_side, flipped)

    return lax.psum_scatter(
        partial_term(jnp.int32(0), row_count * lax.axis_size("col")),
        "col",
        scatter_dimension=0,
        tiled=True,
    )


def norm_forward(inputs, gain, shift):
    full_width = inputs.shape[1] * lax.axis_size("row")
    mean_row = row_totals(jnp.sum(inputs, axis=1)) / full_width
    centred = inputs - mean_row[:, None]
    variance = row_totals(jnp.sum(centred * centred, axis=1)) / full_width
    inv_std = lax.rsqrt(variance + LN_EPS)[:, None]
    normal = centred * inv_std
    return (normal * gain + shift, normal, inv_std)


def norm_backward(upstream, normal, inv_std, gain):
    full_width = upstream.shape[1] * lax.axis_size("row")
    scaled = upstream * gain
    first_sum, second_sum = row_totals((jnp.sum(scaled, axis=1), jnp.sum(scaled * normal, axis=1)))
    grad = inv_std * (
        scaled - first_sum[:, None] / full_width - normal * (second_sum[:, None] / full_width)
    )
    return (grad, jnp.sum(upstream * normal, axis=0), jnp.sum(upstream, axis=0))


def seq_scores(queries, key_rows, segment):
    scaling = HD ** (-0.5)
    scores = (
        jnp.einsum("qhd,khd->hqk", queries, key_rows, preferred_element_type=jnp.float32) * scaling
    )
    same_doc = segment[:, None] == segment[None, :]
    return jnp.where(same_doc[None], scores, MASK_FILL)


def attend_forward(packed, segment):
    scores = seq_scores(packed[:, 0], packed[:, 1], segment)
    row_top = jnp.max(scores, axis=-1, keepdims=True)
    log_total = row_top[..., 0] + jnp.log(jnp.sum(jnp.exp(scores - row_top), axis=-1))
    attn_probs = jnp.exp(scores - log_total[..., None]).astype(jnp.bfloat16)
    context = jnp.einsum(
        "hqk,khd->qhd", attn_probs, packed[:, 2], preferred_element_type=jnp.float32
    )
    return (context.astype(jnp.bfloat16), log_total)


def attend_backward(packed, segment, log_total, grad_context):
    scaling = HD ** (-0.5)
    scores = seq_scores(packed[:, 0], packed[:, 1], segment)
    attn_probs = jnp.exp(scores - log_total[..., None])
    grad_values = jnp.einsum(
        "hqk,qhd->khd",
        attn_probs.astype(jnp.bfloat16),
        grad_context,
        preferred_element_type=jnp.float32,
    )
    grad_probs = jnp.einsum(
        "qhd,khd->hqk", grad_context, packed[:, 2], preferred_element_type=jnp.float32
    )
    inner_sum = jnp.sum(attn_probs * grad_probs, axis=-1, keepdims=True)
    grad_scores = (attn_probs * (grad_probs - inner_sum) * scaling).astype(jnp.bfloat16)
    grad_queries = jnp.einsum(
        "hqk,khd->qhd", grad_scores, packed[:, 1], preferred_element_type=jnp.float32
    )
    grad_keys = jnp.einsum(
        "hqk,qhd->khd", grad_scores, packed[:, 0], preferred_element_type=jnp.float32
    )
    return jnp.stack([grad_queries, grad_keys, grad_values], axis=1)


def adamw(grad, moments):
    first_mom = BETA_ONE * moments[0] + (1.0 - BETA_ONE) * grad
    second_mom = BETA_TWO * moments[1] + (1.0 - BETA_TWO) * grad * grad
    corr_one = 1.0 - BETA_ONE**STEP_COUNT
    corr_two = 1.0 - BETA_TWO**STEP_COUNT
    direction = first_mom / corr_one / (jnp.sqrt(second_mom / corr_two) + ADAM_EPS)
    return (direction, jnp.stack([first_mom, second_mom]))


def body(
    tokens,
    segments,
    cotangent,
    in_proj,
    entry_bias,
    out_proj,
    up_proj,
    hidden_bias,
    down_proj,
    norm_gains,
    row_biases,
    moments_in,
    moments_entry,
    moments_out,
    moments_up,
    moments_hidden,
    moments_down,
    moments_gains,
    moments_biases,
):
    width_here = tokens.shape[1]
    local_width = in_proj.shape[2]
    heads_here = local_width // HD
    seq_count = segments.shape[0]
    seq_len = segments.shape[1]
    in_b = in_proj.reshape(width_here, 3 * local_width).astype(jnp.bfloat16)
    out_b = out_proj.astype(jnp.bfloat16)
    up_b = up_proj.astype(jnp.bfloat16)
    down_b = down_proj.astype(jnp.bfloat16)
    zero_row = jnp.zeros((local_width,), jnp.float32)
    bias_three = rounded(jnp.stack([entry_bias[0], zero_row, entry_bias[1]]))
    tokens_all = spread_cols(tokens)
    mixed_flat = reduce_rows(tokens_all, in_b, False)
    mixed_qkv = mixed_flat.reshape(-1, 3, local_width) + bias_three
    packed = mixed_qkv.astype(jnp.bfloat16).reshape(seq_count, seq_len, 3, heads_here, HD)
    context, log_total = lax.map(
        lambda member: attend_forward(member[0], member[1]), (packed, segments)
    )
    context_flat = context.reshape(-1, local_width)
    context_all = spread_rows(context_flat)
    residual = (
        tokens.astype(jnp.float32) + reduce_cols(context_all, out_b, False) + rounded(row_biases[2])
    )
    normed, normal_one, inv_one = norm_forward(residual, norm_gains[0], row_biases[0])
    normed_b = normed.astype(jnp.bfloat16)
    normed_all = spread_cols(normed_b)
    pre_act = reduce_rows(normed_all, up_b, False) + rounded(hidden_bias)
    hidden_b = gelu_value(pre_act).astype(jnp.bfloat16)
    hidden_all = spread_rows(hidden_b)
    branch = reduce_cols(hidden_all, down_b, False)
    second = normed + branch + rounded(row_biases[3])
    output, normal_two, inv_two = norm_forward(second, norm_gains[1], row_biases[1])
    upstream = cotangent.astype(jnp.float32)
    grad_second, gain_two, shift_two = norm_backward(upstream, normal_two, inv_two, norm_gains[1])
    grad_second_b = grad_second.astype(jnp.bfloat16)
    grad_all = spread_cols(grad_second_b)
    grad_down = outer_sum(hidden_all, grad_all)
    grad_pre = reduce_rows(grad_all, down_b, True) * gelu_slope(pre_act)
    grad_pre_b = grad_pre.astype(jnp.bfloat16)
    grad_hidden = jnp.sum(grad_pre, axis=0)
    grad_pre_all = spread_rows(grad_pre_b)
    grad_up = outer_sum(normed_all, grad_pre_all)
    grad_from_ffn = reduce_cols(grad_pre_all, up_b, True)
    grad_normed = grad_second + grad_from_ffn
    grad_resid, gain_one, shift_one = norm_backward(grad_normed, normal_one, inv_one, norm_gains[0])
    grad_resid_b = grad_resid.astype(jnp.bfloat16)
    grad_resid_all = spread_cols(grad_resid_b)
    grad_out = outer_sum(context_all, grad_resid_all)
    grad_context = reduce_rows(grad_resid_all, out_b, True).astype(jnp.bfloat16)
    grad_context = grad_context.reshape(seq_count, seq_len, heads_here, HD)
    grad_packed = lax.map(
        lambda member: attend_backward(member[0], member[1], member[2], member[3]),
        (packed, segments, log_total, grad_context),
    )
    grad_packed = grad_packed.reshape(-1, 3, local_width)
    grad_entry = jnp.stack([jnp.sum(grad_packed[:, 0], axis=0), jnp.sum(grad_packed[:, 2], axis=0)])
    grad_packed_b = grad_packed.astype(jnp.bfloat16).reshape(-1, 3 * local_width)
    grad_packed_all = spread_rows(grad_packed_b)
    grad_in = outer_sum(tokens_all, grad_packed_all).reshape(width_here, 3, local_width)
    input_grad = (grad_resid + reduce_cols(grad_packed_all, in_b, True)).astype(jnp.bfloat16)
    grad_gains, grad_biases = lax.psum(
        (
            jnp.stack([gain_one, gain_two]),
            jnp.stack(
                [shift_one, shift_two, jnp.sum(grad_resid, axis=0), jnp.sum(grad_second, axis=0)]
            ),
        ),
        ("dp", "col"),
    )
    grad_entry, grad_hidden = lax.psum((grad_entry, grad_hidden), ("dp", "row"))
    grad_in, grad_out, grad_up, grad_down = lax.psum((grad_in, grad_out, grad_up, grad_down), "dp")
    grads = (
        grad_in,
        grad_entry,
        grad_out,
        grad_up,
        grad_hidden,
        grad_down,
        grad_gains,
        grad_biases,
    )
    moments = (
        moments_in,
        moments_entry,
        moments_out,
        moments_up,
        moments_hidden,
        moments_down,
        moments_gains,
        moments_biases,
    )
    updated = [adamw(grad, mom) for grad, mom in zip(grads, moments)]
    return (
        output.astype(jnp.bfloat16),
        input_grad,
        grads[0],
        grads[1],
        grads[2],
        grads[3],
        grads[4],
        grads[5],
        grads[6],
        grads[7],
        updated[0][0],
        updated[1][0],
        updated[2][0],
        updated[3][0],
        updated[4][0],
        updated[5][0],
        updated[6][0],
        updated[7][0],
        updated[0][1],
        updated[1][1],
        updated[2][1],
        updated[3][1],
        updated[4][1],
        updated[5][1],
        updated[6][1],
        updated[7][1],
    )


def solution(mesh):
    in_specs = (
        P(("dp", "col"), "row"),
        P(("dp", "row"), None),
        P(("dp", "col"), "row"),
        P("row", None, "col"),
        P(None, "col"),
        P("col", "row"),
        P("row", "col"),
        P("col"),
        P("col", "row"),
        P(None, "row"),
        P(None, "row"),
        P(None, "row", None, "col"),
        P(None, None, "col"),
        P(None, "col", "row"),
        P(None, "row", "col"),
        P(None, "col"),
        P(None, "col", "row"),
        P(None, None, "row"),
        P(None, None, "row"),
    )
    out_specs = (
        P(("dp", "col"), "row"),
        P(("dp", "col"), "row"),
        P("row", None, "col"),
        P(None, "col"),
        P("col", "row"),
        P("row", "col"),
        P("col"),
        P("col", "row"),
        P(None, "row"),
        P(None, "row"),
        P("row", None, "col"),
        P(None, "col"),
        P("col", "row"),
        P("row", "col"),
        P("col"),
        P("col", "row"),
        P(None, "row"),
        P(None, "row"),
        P(None, "row", None, "col"),
        P(None, None, "col"),
        P(None, "col", "row"),
        P(None, "row", "col"),
        P(None, "col"),
        P(None, "col", "row"),
        P(None, None, "row"),
        P(None, None, "row"),
    )
    return jax.shard_map(body, mesh=mesh, in_specs=in_specs, out_specs=out_specs, check_vma=False)
```

profile of v0, /device:TPU:0, one launch (start us, length us, event | category | flops | bytes accessed | tf_op | source)
XLA Modules:
  0.0 2002.3 jit_solution(1133166957950788562)
XLA Ops:
  9.7 35.8 %all-gather.9.cloned.1.call-done = bf16[4096,256]{1,0:T(8,128)(2,1)} async-done(((bf16[2048,256]{1,0:T(8,128)(2,1)}), bf16[4096,256]{1,0:T(8,128)(2,1)}) %all-gather.9.cloned.1.call-update) | async-done | bytes 2097168 | tf_op jit(solution)/shard_map/all_gather | solution.py:32
  45.4 11.8 fusion.127
  58.2 179.7 %reduce-scatter.9.cloned.1.call-done = f32[1024,1536]{1,0:T(8,128)} async-done(((f32[4096,1536]{1,0:T(8,128)}), f32[1024,1536]{1,0:T(8,128)}) %reduce-scatter.9.cloned.1.call-update) | async-done | bytes 6291472 | tf_op jit(solution)/shard_map/reduce_scatter | solution.py:62
  237.9 6.6 copy.57
  244.5 9.2 reshape.215
  253.6 5.7 add_convert_fusion
  260.1 14.0 while.22
  278.2 34.1 %all-gather.11.cloned.1.call-done = bf16[4096,512]{0,1:T(8,128)(2,1)} async-done(((bf16[1024,512]{0,1:T(8,128)(2,1)}), bf16[4096,512]{0,1:T(8,128)(2,1)}) %all-gather.11.cloned.1.call-update) | async-done | bytes 4194320 | tf_op jit(solution)/shard_map/all_gather | solution.py:36
  312.2 5.6 fusion.103
  318.6 53.7 %reduce-scatter.11.cloned.1.call-done = f32[2048,256]{1,0:T(8,128)} async-done(((f32[4096,256]{1,0:T(8,128)}), f32[2048,256]{1,0:T(8,128)}) %reduce-scatter.11.cloned.1.call-update) | async-done | bytes 2097168 | tf_op jit(solution)/shard_map/reduce_scatter | solution.py:76
  372.3 3.4 fusion.123
  375.8 7.0 psum.112
  385.0 6.0 psum.113
  393.8 32.4 %all-gather.13.cloned.1.call-done = bf16[4096,256]{1,0:T(8,128)(2,1)} async-done(((bf16[2048,256]{1,0:T(8,128)(2,1)}), bf16[4096,256]{1,0:T(8,128)(2,1)}) %all-gather.13.cloned.1.call-update) | async-done | bytes 2097168 | tf_op jit(solution)/shard_map/all_gather | solution.py:32
  426.2 17.8 fusion.94
  444.8 234.4 %reduce-scatter.13.cloned.1.call-done = f32[1024,2048]{1,0:T(8,128)} async-done(((f32[4096,2048]{1,0:T(8,128)}), f32[1024,2048]{1,0:T(8,128)}) %reduce-scatter.13.cloned.1.call-update) | async-done | bytes 8388624 | tf_op jit(solution)/shard_map/reduce_scatter | solution.py:62
  679.2 7.0 multiply_convert_fusion.1
  686.4 105.9 %all-gather.15.cloned.1.call-done = bf16[4096,2048]{1,0:T(8,128)(2,1)} async-done(((bf16[1024,2048]{1,0:T(8,128)(2,1)}), bf16[4096,2048]{1,0:T(8,128)(2,1)}) %all-gather.15.cloned.1.call-update) | async-done | bytes 16777232 | tf_op jit(solution)/shard_map/all_gather | solution.py:36
  792.3 12.9 fusion.90
  805.3 54.4 %reduce-scatter.15.cloned.1.call-done = f32[2048,256]{1,0:T(8,128)} async-done(((f32[4096,256]{1,0:T(8,128)}), f32[2048,256]{1,0:T(8,128)}) %reduce-scatter.15.cloned.1.call-update) | async-done | bytes 2097168 | tf_op jit(solution)/shard_map/reduce_scatter | solution.py:76
  859.7 3.5 fusion.122
  863.2 7.0 psum.114
  872.4 6.1 psum.115
  878.5 3.3 fusion.80
  881.8 10.1 all-reduce.3
  892.0 4.9 fusion.118
  899.5 32.6 %all-gather.17.cloned.1.call-done = bf16[4096,256]{1,0:T(8,128)(2,1)} async-done(((bf16[2048,256]{1,0:T(8,128)(2,1)}), bf16[4096,256]{1,0:T(8,128)(2,1)}) %all-gather.17.cloned.1.call-update) | async-done | bytes 2097168 | tf_op jit(solution)/shard_map/all_gather | solution.py:32
  932.1 17.9 fusion.88
  950.0 235.0 %reduce-scatter.17.cloned.1.call-done = f32[1024,2048]{1,0:T(8,128)} async-done(((f32[4096,2048]{1,0:T(8,128)}), f32[1024,2048]{1,0:T(8,128)}) %reduce-scatter.17.cloned.1.call-update) | async-done | bytes 8388624 | tf_op jit(solution)/shard_map/reduce_scatter | solution.py:62
  1185.0 10.7 fusion.120
  1195.8 106.0 %all-gather.19.cloned.1.call-done = bf16[4096,2048]{1,0:T(8,128)(2,1)} async-done(((bf16[1024,2048]{1,0:T(8,128)(2,1)}), bf16[4096,2048]{1,0:T(8,128)(2,1)}) %all-gather.19.cloned.1.call-update) | async-done | bytes 16777232 | tf_op jit(solution)/shard_map/all_gather | solution.py:36
  1301.8 13.0 fusion.92
  1314.8 54.4 %reduce-scatter.19.cloned.1.call-done = f32[2048,256]{1,0:T(8,128)} async-done(((f32[4096,256]{1,0:T(8,128)}), f32[2048,256]{1,0:T(8,128)}) %reduce-scatter.19.cloned.1.call-update) | async-done | bytes 2097168 | tf_op jit(solution)/shard_map/reduce_scatter | solution.py:76
  1369.3 4.9 multiply_reduce_fusion.1
  1374.2 11.2 all-reduce.2
  1385.3 4.2 fusion.117
  1392.0 32.3 %all-gather.21.cloned.1.call-done = bf16[4096,256]{1,0:T(8,128)(2,1)} async-done(((bf16[2048,256]{1,0:T(8,128)(2,1)}), bf16[4096,256]{1,0:T(8,128)(2,1)}) %all-gather.21.cloned.1.call-update) | async-done | bytes 2097168 | tf_op jit(solution)/shard_map/all_gather | solution.py:32
  1424.3 6.2 fusion.101
  1431.0 71.4 %reduce-scatter.21.cloned.1.call-done = f32[1024,512]{1,0:T(8,128)} async-done(((f32[4096,512]{1,0:T(8,128)}), f32[1024,512]{1,0:T(8,128)}) %reduce-scatter.21.cloned.1.call-update) | async-done | bytes 2097168 | tf_op jit(solution)/shard_map/reduce_scatter | solution.py:62
  1505.1 3.9 reshape.221
  1509.0 3.3 copy.62
  1512.3 91.4 %while.23 = (s32[]{:T(128)}, f32[2,512,3,8,64]{1,4,3,2,0:T(8,128)}, bf16[2,512,3,8,64]{1,4,3,2,0:T(8,128)(2,1)S(1)}, s32[2,512]{1,0:T(2,128)S(1)}, f32[2,8,512]{...) while((s32[]{:T(128)}, f32[2,512,3,8,64]{1,4,3,2,0:T(8,128)}, ...), condition=%wide.region_29.30_spmd, body=%wide.region_27.29_spmd.sunk | while | flops 1398547456 | bytes 173136112 | solution.py:228
  1517.1 3.7 fusion.172
  1520.8 4.5 fusion.173
  1525.3 14.2 fusion.175
  1539.5 14.3 fusion.174
  1553.8 4.1 fusion.176
  1562.7 3.7 fusion.172
  1566.4 4.5 fusion.173
  1570.9 14.2 fusion.175
  1585.1 14.3 fusion.174
  1599.4 4.1 fusion.176
  1603.7 3.3 convert_element_type.114
  1612.8 13.1 fusion.132
  1626.0 11.0 fusion.131
  1639.0 56.0 %all-gather.23.cloned.1.call-done = bf16[4096,1536]{0,1:T(8,128)(2,1)} async-done(((bf16[1024,1536]{0,1:T(8,128)(2,1)}), bf16[4096,1536]{0,1:T(8,128)(2,1)}) %all-gather.23.cloned.1.call-update) | async-done | bytes 12582928 | tf_op jit(solution)/shard_map/all_gather | solution.py:36
  1695.0 7.5 fusion.129
  1706.7 10.3 fusion.128
  1717.8 22.6 %all-reduce.1 = (f32[2,256]{1,0:T(2,128)S(1)}, f32[4,256]{1,0:T(4,128)S(1)}) all-reduce(f32[2,256]{1,0:T(2,128)S(1)} %pad_maximum_fusion.11, f32[4,256]{1,0:T(4,128)S(1)} %pad_maximum_fusion.9), channel_id=1, replica_groups=mesh['dp'=4,'row'=4,'col'=2] {'dp','col'}, use_global_device_ids=true, to_apply=%region_42.43 | all-reduce | flops 1536 | bytes 12288 | tf_op jit(solution)/shard_map/psum | solution.py:238
  1743.0 10.4 copy.65
  1753.3 9.2 reshape.219
  1765.2 61.8 %all-reduce = (f32[2,512]{1,0:T(2,128)S(1)}, f32[2048]{0:T(1024)S(1)}) all-reduce(f32[2,512]{1,0:T(2,128)S(1)} %pad_maximum_fusion.8, f32[2048]{0:T(1024)S(1)} %copy-done.26), channel_id=1, replica_groups=mesh['dp'=4,'row'=4,'col'=2] {'dp','row'}, use_global_device_ids=true, to_apply=%region_34.35 | all-reduce | flops 3072 | bytes 24576 | tf_op jit(solution)/shard_map/psum | solution.py:247
  1829.5 101.4 %all-reduce.7.cloned.1.call-done = (f32[256,3,512]{2,0,1:T(8,128)}, f32[512,256]{1,0:T(8,128)}, f32[256,2048]{1,0:T(8,128)}, f32[2048,256]{1,0:T(8,128)}) async-done(((f32[256,3,512]{2,0,1:T(8,128)}, f32[512,256]{1,0:T(8,128)}, f32[256,2048]{1,0:T(8,128)}, f32[2048,256]{1,0:T(8,128)}), (f32[256,3,512]{2,0,1:T(8,128)}, f32[512,256]{1,0:T(8,128)}, f32[256,2048]{1,0:T(8,128)}, ...) | async-done | bytes 6291472 | tf_op jit(solution)/shard_map/psum | solution.py:248
  1953.2 33.2 %reduce-scatter.23.cloned.1.call-done = f32[2048,256]{1,0:T(8,128)} async-done(((f32[4096,256]{1,0:T(8,128)}), f32[2048,256]{1,0:T(8,128)}) %reduce-scatter.23.cloned.1.call-update) | async-done | bytes 2097168 | tf_op jit(solution)/shard_map/reduce_scatter | solution.py:76
  (223 shorter events, 100.3 us)
Async XLA Ops:
  7.2 38.2 %all-gather.9.cloned.1.call-start = ((), (), s32[]{:S(2)}) async-start(), calls=%async_computation.8 | async-start | bytes 3145728 | tf_op jit(solution)/shard_map/all_gather | solution.py:32
  7.9 229.9 %reduce-scatter.9.cloned.1.call-start = ((), (), s32[]{:S(2)}) async-start(), calls=%async_computation.9 | async-start | bytes 31457280 | tf_op jit(solution)/shard_map/reduce_scatter | solution.py:62
  9.7 47.6 %copy-start.20 = (bf16[256,3,512]{0,2,1:T(8,128)(2,1)}, bf16[256,3,512]{0,2,1:T(8,128)(2,1)S(1)}, u32[]{:S(2)}) copy-start(bf16[256,3,512]{0,2,1:T(8,128)(2,1)S(1)} %copy.56) | copy-start | bytes 2359300
  57.3 254.9 %all-gather.11.cloned.1.call-start = ((), (), s32[]{:S(2)}) async-start(), calls=%async_computation.10 | async-start | bytes 5242880 | tf_op jit(solution)/shard_map/all_gather | solution.py:36
  259.3 0.7 copy-start.25
  262.0 1.8 copy-start.23
  266.1 1.0 copy-start.24
  268.9 1.8 copy-start.23
  273.1 1.0 copy-start.24
  277.6 94.7 %reduce-scatter.11.cloned.1.call-start = ((), (), s32[]{:S(2)}) async-start(), calls=%async_computation.11 | async-start | bytes 6291456 | tf_op jit(solution)/shard_map/reduce_scatter | solution.py:76
  317.8 0.7 copy-start.43
  317.9 108.4 %all-gather.13.cloned.1.call-start = ((), (), s32[]{:S(2)}) async-start(), calls=%async_computation.12 | async-start | bytes 3145728 | tf_op jit(solution)/shard_map/all_gather | solution.py:32
  393.8 285.4 %reduce-scatter.13.cloned.1.call-start = ((), (), s32[]{:S(2)}) async-start(), calls=%async_computation.13 | async-start | bytes 41943040 | tf_op jit(solution)/shard_map/reduce_scatter | solution.py:62
  444.1 348.2 %all-gather.15.cloned.1.call-start = ((), (), s32[]{:S(2)}) async-start(), calls=%async_computation.14 | async-start | bytes 20971520 | tf_op jit(solution)/shard_map/all_gather | solution.py:36
  686.2 173.5 %reduce-scatter.15.cloned.1.call-start = ((), (), s32[]{:S(2)}) async-start(), calls=%async_computation.15 | async-start | bytes 6291456 | tf_op jit(solution)/shard_map/reduce_scatter | solution.py:76
  805.3 126.8 %all-gather.17.cloned.1.call-start = ((), (), s32[]{:S(2)}) async-start(), calls=%async_computation.16 | async-start | bytes 3145728 | tf_op jit(solution)/shard_map/all_gather | solution.py:32
  896.9 1.3 copy-start.3
  899.3 285.7 %reduce-scatter.17.cloned.1.call-start = ((), (), s32[]{:S(2)}) async-start(), calls=%async_computation.17 | async-start | bytes 41943040 | tf_op jit(solution)/shard_map/reduce_scatter | solution.py:62
  950.0 351.8 %all-gather.19.cloned.1.call-start = ((), (), s32[]{:S(2)}) async-start(), calls=%async_computation.18 | async-start | bytes 20971520 | tf_op jit(solution)/shard_map/all_gather | solution.py:36
  1195.7 173.5 %reduce-scatter.19.cloned.1.call-start = ((), (), s32[]{:S(2)}) async-start(), calls=%async_computation.19 | async-start | bytes 6291456 | tf_op jit(solution)/shard_map/reduce_scatter | solution.py:76
  1314.8 109.5 %all-gather.21.cloned.1.call-start = ((), (), s32[]{:S(2)}) async-start(), calls=%async_computation.20 | async-start | bytes 3145728 | tf_op jit(solution)/shard_map/all_gather | solution.py:32
  1389.6 1.3 copy-start.4
  1392.0 110.4 %reduce-scatter.21.cloned.1.call-start = ((), (), s32[]{:S(2)}) async-start(), calls=%async_computation.21 | async-start | bytes 10485760 | tf_op jit(solution)/shard_map/reduce_scatter | solution.py:62
  1430.5 264.5 %all-gather.23.cloned.1.call-start = ((), (), s32[]{:S(2)}) async-start(), calls=%async_computation.22 | async-start | bytes 15728640 | tf_op jit(solution)/shard_map/all_gather | solution.py:36
  1512.3 1.7 copy-start.1
  1515.8 1.3 copy-start.7
  1517.1 3.7 copy-start
  1553.8 4.1 copy-start.2
  1557.9 1.7 copy-start.1
  1561.4 1.3 copy-start.7
  1562.7 3.7 copy-start
  1599.4 4.1 copy-start.2
  1612.8 13.2 copy-start.6
  1612.8 318.1 %all-reduce.7.cloned.1.call-start = ((), (), s32[]{:S(2)}) async-start(), calls=%async_computation.24 | async-start | bytes 12582912 | tf_op jit(solution)/shard_map/psum | solution.py:248
  1626.0 11.0 copy-start.14
  1626.0 11.0 copy-start.18
  1637.0 58.0 %copy-start.17 = (bf16[4096,256]{1,0:T(8,128)(2,1)S(1)}, bf16[4096,256]{1,0:T(8,128)(2,1)}, u32[]{:S(2)}) copy-start(bf16[4096,256]{1,0:T(8,128)(2,1)} %all-gather.9.cloned.1.call-done) | copy-start | bytes 6291460
  1705.6 1.1 copy-start.21
  1705.6 280.8 %reduce-scatter.23.cloned.1.call-start = ((), (), s32[]{:S(2)}) async-start(), calls=%async_computation.23 | async-start | bytes 6291456 | tf_op jit(solution)/shard_map/reduce_scatter | solution.py:76
  1717.0 0.7 copy-start.33
  1717.0 0.7 copy-start.35
  1717.0 0.8 copy-start.34
  1717.0 0.8 copy-start.36
  1717.0 0.8 copy-start.37
  1717.0 0.8 copy-start.38
  1717.1 23.5 %copy-start.39 = (f32[2,2,256]{2,1,0:T(2,128)S(1)}, f32[2,2,256]{2,1,0:T(2,128)}, u32[]{:S(2)}) copy-start(f32[2,2,256]{2,1,0:T(2,128)} %param.40) | copy-start | bytes 12292
  1717.1 24.7 %copy-start.29 = (f32[2,4,256]{2,1,0:T(4,128)S(1)}, f32[2,4,256]{2,1,0:T(4,128)}, u32[]{:S(2)}) copy-start(f32[2,4,256]{2,1,0:T(4,128)} %param.41) | copy-start | bytes 24580
  1740.5 12.8 copy-start.41
  1740.5 12.8 copy-start.44
  1762.5 2.7 copy-start.26
  1762.5 64.4 %copy-start.30 = (f32[2,2,512]{2,1,0:T(2,128)S(1)}, f32[2,2,512]{2,1,0:T(2,128)}, u32[]{:S(2)}) copy-start(f32[2,2,512]{2,1,0:T(2,128)} %param.35) | copy-start | bytes 24580
  1827.0 107.6 %copy-start.32 = (f32[2048]{0:T(1024)}, f32[2048]{0:T(1024)S(1)}, u32[]{:S(2)}) copy-start(f32[2048]{0:T(1024)S(1)} %get-tuple-element.325) | copy-start | bytes 24580
  1827.0 107.6 %copy-start.42 = (f32[2,512]{1,0:T(2,128)}, f32[2,512]{1,0:T(2,128)S(1)}, u32[]{:S(2)}) copy-start(f32[2,512]{1,0:T(2,128)S(1)} %get-tuple-element.322) | copy-start | bytes 12292
  1930.9 3.7 copy-start.12
  1930.9 3.7 copy-start.19
  1936.8 2.3 copy-start.10
  1936.8 4.2 copy-start.15
  1943.6 2.4 copy-start.8
  1943.6 4.5 copy-start.16
  1950.9 35.5 %copy-start.5 = (f32[2048,256]{1,0:T(8,128)S(1)}, f32[2048,256]{1,0:T(8,128)}, u32[]{:S(2)}) copy-start(f32[2048,256]{1,0:T(8,128)} %copy-done.4) | copy-start | bytes 6291460
  1986.4 2.9 copy-start.13
  1989.3 1.4 copy-start.22
  1989.3 2.3 copy-start.11
  1991.6 2.3 copy-start.9
  (4 other events, 2.8 us)
Sparse Core Ops, SparseCore 0:
  9.6 35.8 all-gather.8
  57.4 180.4 reduce-scatter.8
  277.7 34.4 all-gather.10
  318.0 54.3 reduce-scatter.10
  393.9 32.2 all-gather.12
  444.2 234.9 reduce-scatter.12
  686.3 105.9 all-gather.14
  805.4 54.3 reduce-scatter.14
  899.4 32.6 all-gather.16
  950.1 234.8 reduce-scatter.16
  1195.8 105.9 all-gather.18
  1314.9 54.3 reduce-scatter.18
  1392.1 32.1 all-gather.20
  1430.7 71.7 reduce-scatter.20
  1612.9 82.0 all-gather.22
  1705.7 225.1 all-reduce.6
  1933.1 53.1 reduce-scatter.22
where the time goes:
time: 2010 us; the launch traced here: 2000 us
  waiting for transfers between devices  1450 us (72%)
  matrix products  213 us (11%)
  blocking collectives  132 us (7%)
  other arithmetic  104 us (5%)
  local copies, waits for them, and re-layouts  82.4 us (4%)
    reduce_scatter x4, waiting for transfers between devices, reduce_rows(): lax.psum_scatter(partial_term(jnp.int32(0), row_count * lax.axis_size('ro...  721 us
    all_gather x4, waiting for transfers between devices, spread_rows(): return lax.all_gather(block, 'row', axis=0, tiled=True)  302 us
    reduce_scatter x4, waiting for transfers between devices, reduce_cols(): lax.psum_scatter(partial_term(jnp.int32(0), row_count * lax.axis_size('co...  196 us
    all_gather x4, waiting for transfers between devices, spread_cols(): return lax.all_gather(block, 'col', axis=0, tiled=True)  133 us
    psum x1, waiting for transfers between devices, body(): lax.psum((grad_in, grad_out, grad_up, grad_down), 'dp')  101 us
    dot_general x8, matrix products, contract(): lax.dot_general(left_side, right_side, (((1,), right_dim), ((), ())), pre...  95.5 us
    psum x1, blocking collectives, body(): grad_entry, grad_hidden = lax.psum((grad_entry, grad_hidden), ('dp', 'row'))  61.8 us
    psum x6, blocking collectives, row_totals(): return lax.psum(values, 'row')  47.3 us
  transfers between devices with their start and end apart: 17, of which 17 were waited for; matrix products, arithmetic and copies ran while one was open for 4% of the time, Pallas kernels for 0%

commit v1 on v0

--- a/solution.py
+++ b/solution.py
@@ -297,6 +297,289 @@
     )
 
 
+def hop_row(value, k):
+    return lax.ppermute(value, "row", [(r, r ^ k) for r in range(4)])
+
+
+def hop_col(value):
+    return lax.ppermute(value, "col", [(0, 1), (1, 0)])
+
+
+def other_core(value):
+    return hop_row(value, 1)
+
+
+def across_x(value):
+    return hop_row(value, 2)
+
+
+def gather_pieces(own, x_last):
+    by_x = across_x(own)
+    by_y = hop_col(own)
+    both = across_x(by_y) if x_last else hop_col(by_x)
+    grid = {(0, 0): own, (2, 0): by_x, (0, 1): by_y, (2, 1): both}
+    for k, h in list(grid):
+        grid[(k + 1, h)] = other_core(grid[(k, h)])
+    return [[grid[(k, h)] for h in range(2)] for k in range(4)]
+
+
+def gather_rows_small(value):
+    return jnp.concatenate([value] + [hop_row(value, k) for k in (1, 2, 3)], axis=-1)
+
+
+def gather_cols_small(value):
+    return jnp.concatenate([value, hop_col(value)], axis=-1)
+
+
+def to_sequences(tokens, length):
+    me = lax.axis_index("row")
+    parts = []
+    for k in range(4):
+        part = lax.dynamic_slice_in_dim(tokens, (me ^ k) * length, length, axis=0)
+        parts.append(part if k == 0 else hop_row(part, k))
+    return parts
+
+
+def to_columns(blocks, length):
+    me = lax.axis_index("row")
+    out = jnp.zeros((4 * length, blocks[0].shape[1]), blocks[0].dtype)
+    for k in range(4):
+        part = blocks[k] if k == 0 else hop_row(blocks[k], k)
+        out = lax.dynamic_update_slice_in_dim(out, part, (me ^ k) * length, axis=0)
+    return out
+
+
+def chain_sum(value):
+    inward = lax.ppermute(value, "dp", [(0, 1), (3, 2)])
+    half = (value.astype(jnp.float32) + inward.astype(jnp.float32)).astype(jnp.bfloat16)
+    across = lax.ppermute(half, "dp", [(1, 2), (2, 1)])
+    total = (half.astype(jnp.float32) + across.astype(jnp.float32)).astype(jnp.bfloat16)
+    outward = lax.ppermute(total, "dp", [(1, 0), (2, 3)])
+    at = lax.axis_index("dp")
+    return jnp.where((at == 1) | (at == 2), total, outward).astype(jnp.float32)
+
+
+def sum_pieces(make, x_first):
+    def spot(first, second):
+        return (2 * first, second) if x_first else (2 * second, first)
+
+    def first_hop(value):
+        return across_x(value) if x_first else hop_col(value)
+
+    def second_hop(value):
+        return hop_col(value) if x_first else across_x(value)
+
+    def add(first, second, *others):
+        k, h = spot(first, second)
+        total = make(k, h)
+        for other in others:
+            total = total + other.astype(jnp.float32)
+        return total.astype(jnp.bfloat16)
+
+    def near(first, second):
+        k, h = spot(first, second)
+        return other_core(make(k + 1, h).astype(jnp.bfloat16))
+
+    sib = {(a, b): near(a, b) for a, b in ((1, 1), (1, 0), (0, 1), (0, 0))}
+    far = {b: first_hop(add(1, b, sib[(1, b)])) for b in (1, 0)}
+    last = second_hop(add(0, 1, sib[(0, 1)], far[1]))
+    return chain_sum(add(0, 0, sib[(0, 0)], far[0], last))
+
+
+def everyone(value):
+    value = value + lax.ppermute(value, "dp", [(d, d ^ 1) for d in range(4)])
+    return value + lax.ppermute(value, "dp", [(d, d ^ 2) for d in range(4)])
+
+
+def dot(left, right, left_dim=1, right_dim=0):
+    return lax.dot_general(
+        left, right, (((left_dim,), (right_dim,)), ((), ())), preferred_element_type=jnp.float32
+    )
+
+
+def whole_norm(inputs, gain, shift):
+    mean_row = jnp.mean(inputs, axis=1, keepdims=True)
+    centred = inputs - mean_row
+    variance = jnp.mean(centred * centred, axis=1, keepdims=True)
+    inv_std = lax.rsqrt(variance + LN_EPS)
+    normal = centred * inv_std
+    return (normal * gain + shift, normal, inv_std)
+
+
+def whole_norm_backward(upstream, normal, inv_std, gain):
+    scaled = upstream * gain
+    first_mean = jnp.mean(scaled, axis=1, keepdims=True)
+    second_mean = jnp.mean(scaled * normal, axis=1, keepdims=True)
+    grad = inv_std * (scaled - first_mean - normal * second_mean)
+    return (grad, jnp.sum(upstream * normal, axis=0), jnp.sum(upstream, axis=0))
+
+
+def moving_body(
+    tokens,
+    segments,
+    cotangent,
+    in_proj,
+    entry_bias,
+    out_proj,
+    up_proj,
+    hidden_bias,
+    down_proj,
+    norm_gains,
+    row_biases,
+    moments_in,
+    moments_entry,
+    moments_out,
+    moments_up,
+    moments_hidden,
+    moments_down,
+    moments_gains,
+    moments_biases,
+):
+    width = tokens.shape[1]
+    half = in_proj.shape[2]
+    ff_half = up_proj.shape[1]
+    length = segments.shape[1]
+    heads = 2 * half // HD
+    row, col = lax.axis_index("row"), lax.axis_index("col")
+    bf16 = jnp.bfloat16
+
+    x_blocks = to_sequences(tokens, length)
+    w_in = gather_pieces(in_proj.astype(bf16).reshape(width, 3 * half), True)
+    w_out = gather_pieces(out_proj.astype(bf16), False)
+    w_up = gather_pieces(up_proj.astype(bf16), True)
+    w_down = gather_pieces(down_proj.astype(bf16), False)
+    c_blocks = to_sequences(cotangent, length)
+
+    seg_all = lax.all_gather(segments, "row", axis=0, tiled=True)
+    segment = lax.dynamic_index_in_dim(seg_all, col * 4 + row, 0, keepdims=False)
+    wide = gather_rows_small(jnp.concatenate([norm_gains, row_biases], axis=0))
+    gains, biases = wide[:2], wide[2:]
+    entry = gather_cols_small(entry_bias).astype(bf16).astype(jnp.float32)
+    up_bias = gather_cols_small(hidden_bias).astype(bf16).astype(jnp.float32)
+    out_bias = biases[2].astype(bf16).astype(jnp.float32)
+    down_bias = biases[3].astype(bf16).astype(jnp.float32)
+
+    mixed = [sum(dot(x_blocks[k], w_in[k][h]) for k in range(4)) for h in range(2)]
+    mixed = jnp.concatenate([m.reshape(length, 3, half) for m in mixed], axis=2)
+    bias_three = jnp.stack([entry[0], jnp.zeros_like(entry[0]), entry[1]])
+    packed = (mixed + bias_three).astype(bf16).reshape(length, 3, heads, HD)
+    context, log_total = attend_forward(packed, segment)
+    context = context.reshape(length, 2 * half)
+    c_half = [context[:, :half], context[:, half:]]
+    x_all = jnp.concatenate(x_blocks, axis=1)
+    branch = jnp.concatenate(
+        [sum(dot(c_half[h], w_out[k][h]) for h in range(2)) for k in range(4)], axis=1
+    )
+    residual = x_all.astype(jnp.float32) + branch + out_bias
+    normed, normal_one, inv_one = whole_norm(residual, gains[0], biases[0])
+    normed_b = normed.astype(bf16)
+    n_blocks = [normed_b[:, k * width : (k + 1) * width] for k in range(4)]
+    pre = [
+        sum(dot(n_blocks[k], w_up[k][h]) for k in range(4))
+        + up_bias[h * ff_half : (h + 1) * ff_half]
+        for h in range(2)
+    ]
+    hidden = [gelu_value(p).astype(bf16) for p in pre]
+    branch = jnp.concatenate(
+        [sum(dot(hidden[h], w_down[k][h]) for h in range(2)) for k in range(4)], axis=1
+    )
+    second = normed + branch + down_bias
+    output, normal_two, inv_two = whole_norm(second, gains[1], biases[1])
+    output = output.astype(bf16)
+    o_blocks = [output[:, k * width : (k + 1) * width] for k in range(4)]
+    layer_out = to_columns(o_blocks, length)
+
+    upstream = jnp.concatenate(c_blocks, axis=1).astype(jnp.float32)
+    grad_second, gain_two, shift_two = whole_norm_backward(upstream, normal_two, inv_two, gains[1])
+    gs_b = grad_second.astype(bf16)
+    gs_blocks = [gs_b[:, k * width : (k + 1) * width] for k in range(4)]
+    grad_down = sum_pieces(lambda k, h: dot(hidden[h], gs_blocks[k], 0, 0), False)
+    grad_pre = [
+        sum(dot(gs_blocks[k], w_down[k][h], 1, 1) for k in range(4)) * gelu_slope(pre[h])
+        for h in range(2)
+    ]
+    grad_hidden = [jnp.sum(g, axis=0) for g in grad_pre]
+    gp_b = [g.astype(bf16) for g in grad_pre]
+    grad_up = sum_pieces(lambda k, h: dot(n_blocks[k], gp_b[h], 0, 0), True)
+    back = jnp.concatenate(
+        [sum(dot(gp_b[h], w_up[k][h], 1, 1) for h in range(2)) for k in range(4)], axis=1
+    )
+    grad_normed = grad_second + back
+    grad_resid, gain_one, shift_one = whole_norm_backward(
+        grad_normed, normal_one, inv_one, gains[0]
+    )
+    gr_b = grad_resid.astype(bf16)
+    gr_blocks = [gr_b[:, k * width : (k + 1) * width] for k in range(4)]
+    grad_out = sum_pieces(lambda k, h: dot(c_half[h], gr_blocks[k], 0, 0), True)
+    grad_context = jnp.concatenate(
+        [sum(dot(gr_blocks[k], w_out[k][h], 1, 1) for k in range(4)) for h in range(2)], axis=1
+    ).astype(bf16)
+    grad_packed = attend_backward(
+        packed, segment, log_total, grad_context.reshape(length, heads, HD)
+    ).reshape(length, 3, 2 * half)
+    grad_entry = jnp.stack([jnp.sum(grad_packed[:, 0], axis=0), jnp.sum(grad_packed[:, 2], axis=0)])
+    gk_b = grad_packed.astype(bf16)
+    gk_half = [gk_b[:, :, h * half : (h + 1) * half].reshape(length, 3 * half) for h in range(2)]
+    grad_in = sum_pieces(lambda k, h: dot(x_blocks[k], gk_half[h], 0, 0), False)
+    back = [sum(dot(gk_half[h], w_in[k][h], 1, 1) for h in range(2)) for k in range(4)]
+    i_blocks = [
+        (grad_resid[:, k * width : (k + 1) * width] + back[k]).astype(bf16) for k in range(4)
+    ]
+    input_grad = to_columns(i_blocks, length)
+
+    tall = jnp.stack(
+        [
+            gain_one,
+            gain_two,
+            shift_one,
+            shift_two,
+            jnp.sum(grad_resid, axis=0),
+            jnp.sum(grad_second, axis=0),
+        ]
+    )
+    mine = tall[:, :width]
+    for k in (1, 2, 3):
+        mine = mine + hop_row(tall[:, k * width : (k + 1) * width], k)
+    mine = mine + hop_col(mine)
+    own_half = jnp.concatenate([grad_entry[:, :half].reshape(-1), grad_hidden[0]])
+    far_half = jnp.concatenate([grad_entry[:, half:].reshape(-1), grad_hidden[1]])
+    both = own_half + hop_col(far_half)
+    both = both + other_core(both)
+    both = both + across_x(both)
+    flat = everyone(jnp.concatenate([mine.reshape(-1), both]))
+    mine, both = flat[: 6 * width].reshape(6, width), flat[6 * width :]
+    grad_gains, grad_biases = mine[:2], mine[2:]
+    grad_entry, grad_hidden = both[: 2 * half].reshape(2, half), both[2 * half :]
+
+    grads = (
+        grad_in.reshape(width, 3, half),
+        grad_entry,
+        grad_out,
+        grad_up,
+        grad_hidden,
+        grad_down,
+        grad_gains,
+        grad_biases,
+    )
+    moments = (
+        moments_in,
+        moments_entry,
+        moments_out,
+        moments_up,
+        moments_hidden,
+        moments_down,
+        moments_gains,
+        moments_biases,
+    )
+    updated = [adamw(grad, mom) for grad, mom in zip(grads, moments)]
+    return (
+        (layer_out, input_grad)
+        + grads
+        + tuple(u[0] for u in updated)
+        + tuple(u[1] for u in updated)
+    )
+
+
 def solution(mesh):
     in_specs = (
         P(("dp", "col"), "row"),
@@ -347,4 +630,14 @@
         P(None, None, "row"),
         P(None, None, "row"),
     )
-    return jax.shard_map(body, mesh=mesh, in_specs=in_specs, out_specs=out_specs, check_vma=False)
+
+    def step(*args):
+        sizes = dict(mesh.shape)
+        sequences = args[1].shape[0] // (sizes["dp"] * sizes["col"])
+        fits = sizes == {"dp": 4, "row": 4, "col": 2} and sequences == sizes["row"]
+        chosen = moving_body if fits else body
+        return jax.shard_map(
+            chosen, mesh=mesh, in_specs=in_specs, out_specs=out_specs, check_vma=False
+        )(*args)
+
+    return step

time: 2010 us -> 708 us (0.35)
  waiting for transfers between devices: 1450 us -> 222 us
  blocking collectives: 132 us -> 16.3 us
  starting transfers between devices: 2.02 us -> 76.4 us
  other arithmetic: 104 us -> 79.4 us
    reduce_scatter x8 -> x0, waiting for transfers between devices: 916 us -> none  [the longest x4 721 us: reduce_rows(): lax.psum_scatter(partial_term(jnp.int32(0), row_count * lax.axis_size('ro...]
    all_gather x8 -> x0, waiting for transfers between devices: 435 us -> none  [the longest x4 302 us: spread_rows(): return lax.all_gather(block, 'row', axis=0, tiled=True)]
    ppermute x0 -> x94, waiting for transfers between devices: none -> 222 us  [the longest x64 82.2 us: hop_row(): return lax.ppermute(value, 'row', [(r, r ^ k) for r in range(4)])]
    psum x8 -> x0, blocking collectives: 132 us -> none  [the longest x1 61.8 us: body(): grad_entry, grad_hidden = lax.psum((grad_entry, grad_hidden), ('dp', 'row'))]
    psum x1 -> x0, waiting for transfers between devices: 101 us -> none  [body(): lax.psum((grad_in, grad_out, grad_up, grad_down), 'dp')]
    ppermute x0 -> x94, starting transfers between devices: none -> 76.4 us  [the longest x64 31.4 us: hop_row(): return lax.ppermute(value, 'row', [(r, r ^ k) for r in range(4)])]
    reduce_sum x10, other arithmetic: 42 us -> 16.7 us  [the longest x2 4.71 us: whole_norm(): mean_row = jnp.mean(inputs, axis=1, keepdims=True)]
    reshape x4 -> x1, local copies, waits for them, and re-layouts: 25.3 us -> 0.01 us  [moving_body(): flat = everyone(jnp.concatenate([mine.reshape(-1), both]))]
  transfers between devices with their start and end apart: 17 -> 94, of which waited for: 17 -> 29; matrix products, arithmetic and copies ran while one was open for 4% -> 31% of each run, Pallas kernels for 0% -> 0%
where the time goes in v1:
time: 708 us; the launch traced here: 699 us
  matrix products  223 us (31%)
  waiting for transfers between devices  222 us (31%)
  other arithmetic  79.4 us (11%)
  local copies, waits for them, and re-layouts  78.7 us (11%)
  starting transfers between devices  76.4 us (11%)
  blocking collectives  16.3 us (2%)
    dot_general x96, matrix products, dot(): lax.dot_general(left, right, (((left_dim,), (right_dim,)), ((), ())), pre...  138 us
    ppermute x64, waiting for transfers between devices, hop_row(): return lax.ppermute(value, 'row', [(r, r ^ k) for r in range(4)])  82.2 us
    ppermute x16, waiting for transfers between devices, hop_col(): return lax.ppermute(value, 'col', [(0, 1), (1, 0)])  78.3 us
    unnamed x249, local copies, waits for them, and re-layouts  38.6 us
    ppermute x4, waiting for transfers between devices, chain_sum(): inward = lax.ppermute(value, 'dp', [(0, 1), (3, 2)])  31.6 us
    ppermute x64, starting transfers between devices, hop_row(): return lax.ppermute(value, 'row', [(r, r ^ k) for r in range(4)])  31.4 us
    ppermute x4, waiting for transfers between devices, chain_sum(): outward = lax.ppermute(total, 'dp', [(1, 0), (2, 3)])  29.1 us
    dot_general x1, matrix products, attend_backward(): jnp.einsum('hqk,khd->qhd', grad_scores, packed[:, 1], preferred_element_t...  24.9 us
  transfers between devices with their start and end apart: 94, of which 29 were waited for; matrix products, arithmetic and copies ran while one was open for 31% of the time, Pallas kernels for 0%

profile of v1, /device:TPU:0, one launch (start us, length us, event | category | flops | bytes accessed | tf_op | source)
XLA Modules:
  0.0 699.4 jit_solution(14583854001421515120)
XLA Ops:
  0.7 2.7 copy.133
  3.4 3.0 collective-permute-start.6
  11.3 16.3 %all-gather = s32[4,2,512]{2,1,0:T(2,128)S(1)} all-gather(s32[1,2,512]{2,1,0:T(2,128)S(1)} %bitcast.367), channel_id=1, replica_groups=mesh['dp'=4,'row'=4,'col'=2] {'row'}, dimensions={0}, use_global_device_ids=true | all-gather | bytes 20480 | tf_op jit(solution)/shard_map/all_gather | solution.py:453
  29.1 4.2 fusion.232
  42.5 2.7 convert_element_type.363
  53.5 3.1 copy.195
  56.6 3.0 copy.196
  60.1 3.2 collective-permute-done.24
  72.8 4.5 collective-permute-done.1
  79.6 3.4 fusion.245
  85.3 2.8 copy.134
  88.6 11.3 %collective-permute-done.8 = bf16[256,1536]{0,1:T(8,128)(2,1)} collective-permute-done((bf16[256,1536]{0,1:T(8,128)(2,1)}, bf16[256,1536]{0,1:T(8,128)(2,1)}, u32[]{:S(2)}, u32[]{:S(2)}) %collective-permute-start.8) | collective-permute-done | bytes 786464 | tf_op jit(solution)/shard_map/ppermute | solution.py:301
  99.9 2.8 convolution_add_fusion.2
  108.4 3.2 fusion.28
  111.6 7.6 %fusion.4 = (f32[16,512]{1,0:T(8,128)S(1)}, f32[16,512,512]{1,2,0:T(8,128)}) fusion(pred[512,512]{0,1:T(8,128)(4,1)S(1)} %copy-done.51, bf16[512,3,16,64]{0,3,2,1:T(8,128)(2,1)S(1)} %fusion.28), kind=kOutput, calls=%fused_computation.7 | convolution fusion | flops 549445632 | bytes 19169280 | tf_op jit(solution)/shard_map/qhd,khd->hqk/dot_general | solution.py:107
  119.2 9.2 %exponential_reduce_fusion = f32[16,512]{1,0:T(8,128)S(1)} fusion(f32[16,512,512]{1,2,0:T(8,128)} %get-tuple-element.197, f32[16,512]{1,0:T(8,128)S(1)} %get-tuple-element.196, pred[512,512]{0,1:T(8,128)(4,1)} %broadcast_compare_fusion), kind=kLoop, calls=%fused_computation.5 | loop fusion | flops 16769024 | bytes 17104896 | tf_op jit(solution)/shard_map/reduce_sum | solution.py:116
  128.4 8.3 %convolution_convert_fusion.12 = bf16[16,64,512]{2,1,0:T(8,128)(2,1)S(1)} fusion(bf16[512,3,16,64]{0,3,2,1:T(8,128)(2,1)S(1)} %fusion.28, f32[16,512,512]{1,2,0:T(8,128)} %get-tuple-element.197, f32[16,512]{1,0:T(8,128)S(1)} %log_add_fusion, pred[512,512]{0,1:T(8,128)(4,1)} %broadcast_compare_fusion), kind=kOutput, calls=%fused_computation.132 | convolution fusion | flops 554172416 | bytes 19169280 | tf_op jit(solution)/shard_map/hqk,khd->qhd/dot_general | solution.py:118
  141.9 5.6 collective-permute-done.15
  152.9 11.5 %collective-permute-done.22 = bf16[256,2048]{1,0:T(8,128)(2,1)S(1)} collective-permute-done((bf16[256,2048]{1,0:T(8,128)(2,1)}, bf16[256,2048]{1,0:T(8,128)(2,1)S(1)}, u32[]{:S(2)}, u32[]{:S(2)}) %collective-permute-start.22) | collective-permute-done | bytes 1048608 | tf_op jit(solution)/shard_map/ppermute | solution.py:301
  164.9 3.4 fusion.228
  175.2 11.8 %collective-permute-done.32 = bf16[2048,256]{1,0:T(8,128)(2,1)S(1)} collective-permute-done((bf16[2048,256]{1,0:T(8,128)(2,1)S(1)}, bf16[2048,256]{1,0:T(8,128)(2,1)S(1)}, u32[]{:S(2)}, u32[]{:S(2)}) %collective-permute-start.32) | collective-permute-done | bytes 1048608 | tf_op jit(solution)/shard_map/ppermute | solution.py:301
  189.9 19.1 %collective-permute-done.27 = bf16[256,2048]{1,0:T(8,128)(2,1)S(1)} collective-permute-done((bf16[256,2048]{1,0:T(8,128)(2,1)}, bf16[256,2048]{1,0:T(8,128)(2,1)S(1)}, u32[]{:S(2)}, u32[]{:S(2)}) %collective-permute-start.27) | collective-permute-done | bytes 1048608 | tf_op jit(solution)/shard_map/ppermute | solution.py:301
  217.5 16.3 %collective-permute-done.33 = bf16[2048,256]{1,0:T(8,128)(2,1)S(1)} collective-permute-done((bf16[2048,256]{1,0:T(8,128)(2,1)S(1)}, bf16[2048,256]{1,0:T(8,128)(2,1)S(1)}, u32[]{:S(2)}, u32[]{:S(2)}) %collective-permute-start.33) | collective-permute-done | bytes 1048608 | tf_op jit(solution)/shard_map/ppermute | solution.py:305
  234.3 3.5 multiply_convert_fusion.1
  244.1 3.2 fusion.222
  250.5 3.6 fusion.230
  254.2 2.7 fusion.250
  260.2 2.8 fusion.251
  266.1 4.4 fusion.231
  270.6 2.8 convolution_add_fusion.17
  276.9 3.3 multiply_reduce_fusion.1
  288.1 9.4 %fusion.66 = f32[16,512,512]{1,2,0:T(8,128)} fusion(bf16[512,3,16,64]{0,3,2,1:T(8,128)(2,1)} %copy-done.15, bf16[512,8,64]{0,2,1:T(8,128)(2,1)S(1)} %bitcast.337, bf16[512,8,64]{0,2,1:T(8,128)(2,1)S(1)} %bitcast.335), kind=kOutput, calls=%fused_computation.170 | convolution fusion | flops 537395200 | bytes 18874368 | tf_op jit(solution)/shard_map/qhd,khd->hqk/dot_general | solution.py:134
  297.5 10.1 %bitcast_convert_fusion = (bf16[512,16,64]{0,2,1:T(8,128)(2,1)}, f32[16,64,512]{2,1,0:T(8,128)}) fusion(f32[16,512,512]{1,2,0:T(8,128)} %get-tuple-element.197, f32[16,512]{1,0:T(8,128)S(1)} %log_add_fusion, pred[512,512]{0,1:T(8,128)(4,1)S(1)} %copy-done.52, bf16[512,8,64]{0,2,1:T(8,128)(2,1)S(1)} %bitcast.338, bf16[512,8,64]{0,2,1:T(8,128)(2,1)S(1)} %bitcast.336), kind=kOutput, calls=%fused_computation.90 | convolution fusion | flops 554696704 | bytes 21266432 | tf_op jit(solution)/shard_map/hqk,qhd->khd/dot_general | solution.py:128
  335.1 24.9 %bitcast_convert_fusion.1 = (bf16[512,16,64]{0,2,1:T(8,128)(2,1)S(1)}, f32[16,64,512]{2,1,0:T(8,128)}) fusion(f32[16,512,512]{1,2,0:T(8,128)} %fusion.66, f32[16,512,512]{1,2,0:T(8,128)} %get-tuple-element.197, f32[16,512]{1,0:T(8,128)S(1)} %log_add_fusion, pred[512,512]{0,1:T(8,128)(4,1)S(1)} %copy-done.52, bf16[512,3,16,64]{0,3,2,1:T(8,128)(2,1)} %copy-done.15), kind=kOutput, calls=%fused_computation.92 | convolution fusion | flops 583541248 | bytes 71892992 | tf_op jit(solution)/shard_map/hqk,khd->qhd/dot_general | solution.py:139
  360.0 24.8 %fusion.61 = bf16[16,64,512]{2,1,0:T(8,128)(2,1)} fusion(f32[16,512,512]{1,2,0:T(8,128)} %fusion.66, f32[16,512,512]{1,2,0:T(8,128)} %get-tuple-element.197, f32[16,512]{1,0:T(8,128)S(1)} %log_add_fusion, pred[512,512]{0,1:T(8,128)(4,1)S(1)} %copy-done.52, bf16[512,3,16,64]{0,3,2,1:T(8,128)(2,1)} %copy-done.15), kind=kOutput, calls=%fused_computation.131 | convolution fusion | flops 583541248 | bytes 69795840 | tf_op jit(solution)/shard_map/hqk,qhd->khd/dot_general | solution.py:142
  390.2 2.5 convolution_bitcast_fusion
  421.9 3.1 fusion.72
  436.6 2.6 collective-permute-start.63
  478.4 3.8 collective-permute-done.66
  482.3 2.9 collective-permute-done.70
  485.9 2.4 add_convert_fusion.5
  488.3 3.7 collective-permute-start.71
  492.8 4.9 collective-permute-done.71
  501.7 16.5 %collective-permute-done.50 = bf16[256,1536]{1,0:T(8,128)(2,1)S(1)} collective-permute-done((bf16[256,1536]{1,0:T(8,128)(2,1)S(1)}, bf16[256,1536]{1,0:T(8,128)(2,1)S(1)}, u32[]{:S(2)}, u32[]{:S(2)}) %collective-permute-start.50) | collective-permute-done | bytes 786464 | tf_op jit(solution)/shard_map/ppermute | solution.py:305
  521.6 4.9 collective-permute-done.73
  529.9 5.2 collective-permute-done.47
  537.2 18.5 %collective-permute-done.89 = bf16[2048,256]{1,0:T(8,128)(2,1)S(1)} collective-permute-done((bf16[2048,256]{1,0:T(8,128)(2,1)S(1)}, bf16[2048,256]{1,0:T(8,128)(2,1)S(1)}, u32[]{:S(2)}, u32[]{:S(2)}) %collective-permute-start.89) | collective-permute-done | bytes 1048608 | tf_op jit(solution)/shard_map/ppermute | solution.py:305
  555.7 4.4 collective-permute-start.52
  564.2 11.0 %collective-permute-done.52 = bf16[256,1536]{1,0:T(8,128)(2,1)S(1)} collective-permute-done((bf16[256,1536]{1,0:T(8,128)(2,1)S(1)}, bf16[256,1536]{1,0:T(8,128)(2,1)S(1)}, u32[]{:S(2)}, u32[]{:S(2)}) %collective-permute-start.52) | collective-permute-done | bytes 786464 | tf_op jit(solution)/shard_map/ppermute | solution.py:353
  576.5 10.2 %collective-permute-done.86 = bf16[2048,256]{1,0:T(8,128)(2,1)S(1)} collective-permute-done((bf16[2048,256]{1,0:T(8,128)(2,1)S(1)}, bf16[2048,256]{1,0:T(8,128)(2,1)S(1)}, u32[]{:S(2)}, u32[]{:S(2)}) %collective-permute-start.86) | collective-permute-done | bytes 1048608 | tf_op jit(solution)/shard_map/ppermute | solution.py:305
  588.1 3.9 collective-permute-start.91
  592.0 14.8 %collective-permute-done.76 = bf16[256,2048]{1,0:T(8,128)(2,1)S(1)} collective-permute-done((bf16[256,2048]{1,0:T(8,128)(2,1)S(1)}, bf16[256,2048]{1,0:T(8,128)(2,1)S(1)}, u32[]{:S(2)}, u32[]{:S(2)}) %collective-permute-start.76) | collective-permute-done | bytes 1048608 | tf_op jit(solution)/shard_map/ppermute | solution.py:301
  607.5 4.4 collective-permute-start.81
  616.3 15.7 %collective-permute-done.81 = bf16[256,2048]{1,0:T(8,128)(2,1)S(1)} collective-permute-done((bf16[256,2048]{1,0:T(8,128)(2,1)S(1)}, bf16[256,2048]{1,0:T(8,128)(2,1)S(1)}, u32[]{:S(2)}, u32[]{:S(2)}) %collective-permute-start.81) | collective-permute-done | bytes 1048608 | tf_op jit(solution)/shard_map/ppermute | solution.py:353
  640.1 2.8 add_convert_fusion
  646.1 3.7 copy.172
  651.4 3.5 fusion.58
  654.9 3.0 copy.171
  661.1 11.8 %collective-permute-done.93 = bf16[2048,256]{1,0:T(8,128)(2,1)} collective-permute-done((bf16[2048,256]{1,0:T(8,128)(2,1)}, bf16[2048,256]{1,0:T(8,128)(2,1)}, u32[]{:S(2)}, u32[]{:S(2)}) %collective-permute-start.93) | collective-permute-done | bytes 1048608 | tf_op jit(solution)/shard_map/ppermute | solution.py:357
  672.9 2.4 fusion.70
  676.1 2.6 fusion.76
  678.7 12.4 %collective-permute-done.83 = bf16[256,2048]{1,0:T(8,128)(2,1)S(1)} collective-permute-done((bf16[256,2048]{1,0:T(8,128)(2,1)S(1)}, bf16[256,2048]{1,0:T(8,128)(2,1)S(1)}, u32[]{:S(2)}, u32[]{:S(2)}) %collective-permute-start.83) | collective-permute-done | bytes 1048608 | tf_op jit(solution)/shard_map/ppermute | solution.py:357
  691.8 2.6 fusion.77
  696.7 2.5 pad_maximum_fusion
  (607 shorter events, 258.8 us)
Async XLA Ops:
  3.4 66.6 %collective-permute-start.6 = (bf16[256,1536]{0,1:T(8,128)(2,1)}, bf16[256,1536]{0,1:T(8,128)(2,1)}, u32[]{:S(2)}, u32[]{:S(2)}) collective-permute-start(bf16[256,1536]{0,1:T(8,128)(2,1)} %bitcast), channel_id=1, source_target_pairs={{0,1},{1,0},{2,3},{3,2},{4,5},{5,4},{6,7},{7,6},{8,9},{9,8},{10,11... | collective-permute-start | bytes 2359304 | tf_op jit(solution)/shard_map/ppermute | solution.py:305
  6.3 64.1 %collective-permute-start.3 = (bf16[256,1536]{0,1:T(8,128)(2,1)}, bf16[256,1536]{0,1:T(8,128)(2,1)}, u32[]{:S(2)}, u32[]{:S(2)}) collective-permute-start(bf16[256,1536]{0,1:T(8,128)(2,1)} %bitcast), channel_id=1, source_target_pairs={{0,2},{2,0},{4,6},{6,4},{1,3},{3,1},{5,7},{7,5},{8,10},{10,8},{12,... | collective-permute-start | bytes 2359304 | tf_op jit(solution)/shard_map/ppermute | solution.py:301
  6.3 64.2 %collective-permute-start.4 = (bf16[256,1536]{0,1:T(8,128)(2,1)}, bf16[256,1536]{0,1:T(8,128)(2,1)}, u32[]{:S(2)}, u32[]{:S(2)}) collective-permute-start(bf16[256,1536]{0,1:T(8,128)(2,1)} %bitcast), channel_id=1, source_target_pairs={{0,4},{2,6},{4,0},{6,2},{1,5},{3,7},{5,1},{7,3},{8,12},{10,14},{12... | collective-permute-start | bytes 2359304 | tf_op jit(solution)/shard_map/ppermute | solution.py:301
  7.8 51.8 %collective-permute-start.10 = (bf16[2,512]{1,0:T(2,128)(2,1)S(1)}, bf16[2,512]{1,0:T(2,128)(2,1)S(1)}, u32[]{:S(2)}, u32[]{:S(2)}) collective-permute-start(bf16[2,512]{1,0:T(2,128)(2,1)S(1)} %convert.62), channel_id=1, source_target_pairs={{0,1},{1,0},{2,3},{3,2},{4,5},{5,4},{6,7},{7,6},{8,9},{9,8},{10,11... | collective-permute-start | bytes 6152 | tf_op jit(solution)/shard_map/ppermute | solution.py:305
  8.4 56.4 %collective-permute-start.18 = (f32[6,256]{1,0:T(8,128)S(1)}, f32[6,256]{1,0:T(8,128)S(1)}, u32[]{:S(2)}, u32[]{:S(2)}) collective-permute-start(f32[6,256]{1,0:T(8,128)S(1)} %pad_maximum_fusion.14), channel_id=1, source_target_pairs={{0,2},{2,0},{4,6},{6,4},{1,3},{3,1},{5,7},{7,5},{8,10},{10,8},{12,... | collective-permute-start | bytes 18440 | tf_op jit(solution)/shard_map/ppermute | solution.py:301
  68.7 14.3 %collective-permute-start.2 = (bf16[512,256]{0,1:T(8,128)(2,1)}, bf16[512,256]{0,1:T(8,128)(2,1)S(1)}, u32[]{:S(2)}, u32[]{:S(2)}) collective-permute-start(bf16[512,256]{0,1:T(8,128)(2,1)} %copy.190), channel_id=1, source_target_pairs={{0,6},{2,4},{4,2},{6,0},{1,7},{3,5},{5,3},{7,1},{8,14},{10,12},{12... | collective-permute-start | bytes 786440 | tf_op jit(solution)/shard_map/ppermute | solution.py:301
  70.0 68.3 %collective-permute-start.11 = (bf16[512,256]{1,0:T(8,128)(2,1)}, bf16[512,256]{1,0:T(8,128)(2,1)}, u32[]{:S(2)}, u32[]{:S(2)}) collective-permute-start(bf16[512,256]{1,0:T(8,128)(2,1)} %convert_element_type.361), channel_id=1, source_target_pairs={{0,1},{1,0},{2,3},{3,2},{4,5},{5,4},{6,7},{7,6},{8,9},{9,8},{10,11... | collective-permute-start | bytes 786440 | tf_op jit(solution)/shard_map/ppermute | solution.py:305
  70.4 17.7 %collective-permute-start.7 = (bf16[256,1536]{0,1:T(8,128)(2,1)}, bf16[256,1536]{0,1:T(8,128)(2,1)}, u32[]{:S(2)}, u32[]{:S(2)}) collective-permute-start(bf16[256,1536]{0,1:T(8,128)(2,1)} %collective-permute-done.6), channel_id=1, source_target_pairs={{0,2},{2,0},{4,6},{6,4},{1,3},{3,1},{5,7},{7,5},{8,10},{10,8},{12,... | collective-permute-start | bytes 2359304 | tf_op jit(solution)/shard_map/ppermute | solution.py:301
  77.3 22.6 %collective-permute-start.8 = (bf16[256,1536]{0,1:T(8,128)(2,1)}, bf16[256,1536]{0,1:T(8,128)(2,1)}, u32[]{:S(2)}, u32[]{:S(2)}) collective-permute-start(bf16[256,1536]{0,1:T(8,128)(2,1)} %collective-permute-done.6), channel_id=1, source_target_pairs={{0,4},{2,6},{4,0},{6,2},{1,5},{3,7},{5,1},{7,3},{8,12},{10,14},{12... | collective-permute-start | bytes 2359304 | tf_op jit(solution)/shard_map/ppermute | solution.py:301
  83.0 64.8 %collective-permute-start.12 = (bf16[512,256]{1,0:T(8,128)(2,1)}, bf16[512,256]{1,0:T(8,128)(2,1)}, u32[]{:S(2)}, u32[]{:S(2)}) collective-permute-start(bf16[512,256]{1,0:T(8,128)(2,1)} %convert_element_type.361), channel_id=1, source_target_pairs={{0,2},{2,0},{4,6},{6,4},{1,3},{3,1},{5,7},{7,5},{8,10},{10,8},{12,... | collective-permute-start | bytes 786440 | tf_op jit(solution)/shard_map/ppermute | solution.py:301
  83.0 55.8 %collective-permute-start.14 = (bf16[512,256]{1,0:T(8,128)(2,1)}, bf16[512,256]{1,0:T(8,128)(2,1)}, u32[]{:S(2)}, u32[]{:S(2)}) collective-permute-start(bf16[512,256]{1,0:T(8,128)(2,1)} %convert_element_type.361), channel_id=1, source_target_pairs={{0,4},{2,6},{4,0},{6,2},{1,5},{3,7},{5,1},{7,3},{8,12},{10,14},{12... | collective-permute-start | bytes 786440 | tf_op jit(solution)/shard_map/ppermute | solution.py:301
  88.1 84.0 %collective-permute-start.25 = (bf16[256,2048]{1,0:T(8,128)(2,1)}, bf16[256,2048]{1,0:T(8,128)(2,1)}, u32[]{:S(2)}, u32[]{:S(2)}) collective-permute-start(bf16[256,2048]{1,0:T(8,128)(2,1)} %convert_element_type.363), channel_id=1, source_target_pairs={{0,1},{1,0},{2,3},{3,2},{4,5},{5,4},{6,7},{7,6},{8,9},{9,8},{10,11... | collective-permute-start | bytes 3145736 | tf_op jit(solution)/shard_map/ppermute | solution.py:305
  104.5 68.2 %collective-permute-start.21 = (bf16[256,2048]{1,0:T(8,128)(2,1)}, bf16[256,2048]{1,0:T(8,128)(2,1)}, u32[]{:S(2)}, u32[]{:S(2)}) collective-permute-start(bf16[256,2048]{1,0:T(8,128)(2,1)} %convert_element_type.363), channel_id=1, source_target_pairs={{0,2},{2,0},{4,6},{6,4},{1,3},{3,1},{5,7},{7,5},{8,10},{10,8},{12,... | collective-permute-start | bytes 3145736 | tf_op jit(solution)/shard_map/ppermute | solution.py:301
  138.2 26.2 %collective-permute-start.22 = (bf16[256,2048]{1,0:T(8,128)(2,1)}, bf16[256,2048]{1,0:T(8,128)(2,1)S(1)}, u32[]{:S(2)}, u32[]{:S(2)}) collective-permute-start(bf16[256,2048]{1,0:T(8,128)(2,1)} %convert_element_type.363), channel_id=1, source_target_pairs={{0,4},{2,6},{4,0},{6,2},{1,5},{3,7},{5,1},{7,3},{8,12},{10,14},{12... | collective-permute-start | bytes 3145736 | tf_op jit(solution)/shard_map/ppermute | solution.py:301
  150.5 66.1 %collective-permute-start.29 = (bf16[2048,256]{1,0:T(8,128)(2,1)S(1)}, bf16[2048,256]{1,0:T(8,128)(2,1)S(1)}, u32[]{:S(2)}, u32[]{:S(2)}) collective-permute-start(bf16[2048,256]{1,0:T(8,128)(2,1)S(1)} %copy-done.42), channel_id=1, source_target_pairs={{0,1},{1,0},{2,3},{3,2},{4,5},{5,4},{6,7},{7,6},{8,9},{9,8},{10,11... | collective-permute-start | bytes 3145736 | tf_op jit(solution)/shard_map/ppermute | solution.py:305
  151.4 35.6 %collective-permute-start.32 = (bf16[2048,256]{1,0:T(8,128)(2,1)S(1)}, bf16[2048,256]{1,0:T(8,128)(2,1)S(1)}, u32[]{:S(2)}, u32[]{:S(2)}) collective-permute-start(bf16[2048,256]{1,0:T(8,128)(2,1)S(1)} %copy-done.42), channel_id=1, source_target_pairs={{0,4},{2,6},{4,0},{6,2},{1,5},{3,7},{5,1},{7,3},{8,12},{10,14},{12... | collective-permute-start | bytes 3145736 | tf_op jit(solution)/shard_map/ppermute | solution.py:301
  164.5 22.5 %collective-permute-start.23 = (bf16[256,2048]{1,0:T(8,128)(2,1)S(1)}, bf16[256,2048]{1,0:T(8,128)(2,1)S(1)}, u32[]{:S(2)}, u32[]{:S(2)}) collective-permute-start(bf16[256,2048]{1,0:T(8,128)(2,1)S(1)} %collective-permute-done.22), channel_id=1, source_target_pairs={{0,2},{2,0},{4,6},{6,4},{1,3},{3,1},{5,7},{7,5},{8,10},{10,8},{12,... | collective-permute-start | bytes 3145736 | tf_op jit(solution)/shard_map/ppermute | solution.py:301
  172.1 38.9 %collective-permute-start.30 = (bf16[2048,256]{1,0:T(8,128)(2,1)S(1)}, bf16[2048,256]{1,0:T(8,128)(2,1)S(1)}, u32[]{:S(2)}, u32[]{:S(2)}) collective-permute-start(bf16[2048,256]{1,0:T(8,128)(2,1)S(1)} %copy-done.42), channel_id=1, source_target_pairs={{0,2},{2,0},{4,6},{6,4},{1,3},{3,1},{5,7},{7,5},{8,10},{10,8},{12,... | collective-permute-start | bytes 3145736 | tf_op jit(solution)/shard_map/ppermute | solution.py:301
  172.7 36.3 %collective-permute-start.27 = (bf16[256,2048]{1,0:T(8,128)(2,1)}, bf16[256,2048]{1,0:T(8,128)(2,1)S(1)}, u32[]{:S(2)}, u32[]{:S(2)}) collective-permute-start(bf16[256,2048]{1,0:T(8,128)(2,1)} %collective-permute-done.25), channel_id=1, source_target_pairs={{0,4},{2,6},{4,0},{6,2},{1,5},{3,7},{5,1},{7,3},{8,12},{10,14},{12... | collective-permute-start | bytes 3145736 | tf_op jit(solution)/shard_map/ppermute | solution.py:301
  186.9 28.3 %collective-permute-start.26 = (bf16[256,2048]{1,0:T(8,128)(2,1)}, bf16[256,2048]{1,0:T(8,128)(2,1)S(1)}, u32[]{:S(2)}, u32[]{:S(2)}) collective-permute-start(bf16[256,2048]{1,0:T(8,128)(2,1)} %collective-permute-done.25), channel_id=1, source_target_pairs={{0,2},{2,0},{4,6},{6,4},{1,3},{3,1},{5,7},{7,5},{8,10},{10,8},{12,... | collective-permute-start | bytes 3145736 | tf_op jit(solution)/shard_map/ppermute | solution.py:301
  186.9 25.0 %collective-permute-start.34 = (bf16[2048,256]{1,0:T(8,128)(2,1)S(1)}, bf16[2048,256]{1,0:T(8,128)(2,1)S(1)}, u32[]{:S(2)}, u32[]{:S(2)}) collective-permute-start(bf16[2048,256]{1,0:T(8,128)(2,1)S(1)} %collective-permute-done.32), channel_id=1, source_target_pairs={{0,2},{2,0},{4,6},{6,4},{1,3},{3,1},{5,7},{7,5},{8,10},{10,8},{12,... | collective-permute-start | bytes 3145736 | tf_op jit(solution)/shard_map/ppermute | solution.py:301
  209.0 24.8 %collective-permute-start.33 = (bf16[2048,256]{1,0:T(8,128)(2,1)S(1)}, bf16[2048,256]{1,0:T(8,128)(2,1)S(1)}, u32[]{:S(2)}, u32[]{:S(2)}) collective-permute-start(bf16[2048,256]{1,0:T(8,128)(2,1)S(1)} %collective-permute-done.32), channel_id=1, source_target_pairs={{0,1},{1,0},{2,3},{3,2},{4,5},{5,4},{6,7},{7,6},{8,9},{9,8},{10,11... | collective-permute-start | bytes 3145736 | tf_op jit(solution)/shard_map/ppermute | solution.py:305
  211.1 22.8 %collective-permute-start.28 = (bf16[256,2048]{1,0:T(8,128)(2,1)S(1)}, bf16[256,2048]{1,0:T(8,128)(2,1)S(1)}, u32[]{:S(2)}, u32[]{:S(2)}) collective-permute-start(bf16[256,2048]{1,0:T(8,128)(2,1)S(1)} %collective-permute-done.27), channel_id=1, source_target_pairs={{0,2},{2,0},{4,6},{6,4},{1,3},{3,1},{5,7},{7,5},{8,10},{10,8},{12,... | collective-permute-start | bytes 3145736 | tf_op jit(solution)/shard_map/ppermute | solution.py:301
  211.9 31.0 %collective-permute-start.39 = (bf16[512,256]{0,1:T(8,128)(2,1)}, bf16[512,256]{0,1:T(8,128)(2,1)S(1)}, u32[]{:S(2)}, u32[]{:S(2)}) collective-permute-start(bf16[512,256]{0,1:T(8,128)(2,1)} %copy.192), channel_id=1, source_target_pairs={{0,2},{2,0},{4,6},{6,4},{1,3},{3,1},{5,7},{7,5},{8,10},{10,8},{12,... | collective-permute-start | bytes 786440 | tf_op jit(solution)/shard_map/ppermute | solution.py:301
  215.3 27.7 %collective-permute-start.40 = (bf16[512,256]{0,1:T(8,128)(2,1)}, bf16[512,256]{0,1:T(8,128)(2,1)S(1)}, u32[]{:S(2)}, u32[]{:S(2)}) collective-permute-start(bf16[512,256]{0,1:T(8,128)(2,1)} %copy.193), channel_id=1, source_target_pairs={{0,4},{2,6},{4,0},{6,2},{1,5},{3,7},{5,1},{7,3},{8,12},{10,14},{12... | collective-permute-start | bytes 786440 | tf_op jit(solution)/shard_map/ppermute | solution.py:301
  216.5 26.4 %collective-permute-start.41 = (bf16[512,256]{0,1:T(8,128)(2,1)S(1)}, bf16[512,256]{0,1:T(8,128)(2,1)S(1)}, u32[]{:S(2)}, u32[]{:S(2)}) collective-permute-start(bf16[512,256]{0,1:T(8,128)(2,1)S(1)} %copy-done.95), channel_id=1, source_target_pairs={{0,6},{2,4},{4,2},{6,0},{1,7},{3,5},{5,3},{7,1},{8,14},{10,12},{12... | collective-permute-start | bytes 786440 | tf_op jit(solution)/shard_map/ppermute | solution.py:301
  392.8 33.6 %collective-permute-start.55 = (f32[6,256]{1,0:T(8,128)S(1)}, f32[6,256]{1,0:T(8,128)S(1)}, u32[]{:S(2)}, u32[]{:S(2)}) collective-permute-start(f32[6,256]{1,0:T(8,128)S(1)} %get-tuple-element.164), channel_id=1, source_target_pairs={{0,2},{2,0},{4,6},{6,4},{1,3},{3,1},{5,7},{7,5},{8,10},{10,8},{12,... | collective-permute-start | bytes 18440 | tf_op jit(solution)/shard_map/ppermute | solution.py:301
  392.9 33.6 %collective-permute-start.56 = (f32[6,256]{1,0:T(8,128)S(1)}, f32[6,256]{1,0:T(8,128)S(1)}, u32[]{:S(2)}, u32[]{:S(2)}) collective-permute-start(f32[6,256]{1,0:T(8,128)S(1)} %get-tuple-element.166), channel_id=1, source_target_pairs={{0,4},{2,6},{4,0},{6,2},{1,5},{3,7},{5,1},{7,3},{8,12},{10,14},{12... | collective-permute-start | bytes 18440 | tf_op jit(solution)/shard_map/ppermute | solution.py:301
  393.4 33.5 %collective-permute-start.57 = (f32[6,256]{1,0:T(8,128)S(1)}, f32[6,256]{1,0:T(8,128)S(1)}, u32[]{:S(2)}, u32[]{:S(2)}) collective-permute-start(f32[6,256]{1,0:T(8,128)S(1)} %get-tuple-element.165), channel_id=1, source_target_pairs={{0,6},{2,4},{4,2},{6,0},{1,7},{3,5},{5,3},{7,1},{8,14},{10,12},{12... | collective-permute-start | bytes 18440 | tf_op jit(solution)/shard_map/ppermute | solution.py:301
  398.5 27.4 %collective-permute-start.59 = (f32[3072]{0:T(1024)S(1)}, f32[3072]{0:T(1024)S(1)}, u32[]{:S(2)}, u32[]{:S(2)}) collective-permute-start(f32[3072]{0:T(1024)S(1)} %pad_maximum_fusion.13), channel_id=1, source_target_pairs={{0,1},{1,0},{2,3},{3,2},{4,5},{5,4},{6,7},{7,6},{8,9},{9,8},{10,11... | collective-permute-start | bytes 36872 | tf_op jit(solution)/shard_map/ppermute | solution.py:305
  399.1 86.2 %collective-permute-start.85 = (bf16[2048,256]{1,0:T(8,128)(2,1)}, bf16[2048,256]{1,0:T(8,128)(2,1)}, u32[]{:S(2)}, u32[]{:S(2)}) collective-permute-start(bf16[2048,256]{1,0:T(8,128)(2,1)} %convolution_convert_fusion.2), channel_id=1, source_target_pairs={{0,2},{2,0},{4,6},{6,4},{1,3},{3,1},{5,7},{7,5},{8,10},{10,8},{12,... | collective-permute-start | bytes 3145736 | tf_op jit(solution)/shard_map/ppermute | solution.py:301
  425.9 20.5 %collective-permute-start.68 = (bf16[512,256]{1,0:T(8,128)(2,1)}, bf16[512,256]{1,0:T(8,128)(2,1)}, u32[]{:S(2)}, u32[]{:S(2)}) collective-permute-start(bf16[512,256]{1,0:T(8,128)(2,1)} %convolution_convert_fusion.13), channel_id=1, source_target_pairs={{0,2},{2,0},{4,6},{6,4},{1,3},{3,1},{5,7},{7,5},{8,10},{10,8},{12,... | collective-permute-start | bytes 786440 | tf_op jit(solution)/shard_map/ppermute | solution.py:301
  426.4 22.9 %collective-permute-start.42 = (bf16[512,256]{0,1:T(8,128)(2,1)}, bf16[512,256]{0,1:T(8,128)(2,1)}, u32[]{:S(2)}, u32[]{:S(2)}) collective-permute-start(bf16[512,256]{0,1:T(8,128)(2,1)} %get-tuple-element.146), channel_id=1, source_target_pairs={{0,2},{2,0},{4,6},{6,4},{1,3},{3,1},{5,7},{7,5},{8,10},{10,8},{12,... | collective-permute-start | bytes 786440 | tf_op jit(solution)/shard_map/ppermute | solution.py:301
  431.2 20.7 %collective-permute-start.43 = (bf16[512,256]{0,1:T(8,128)(2,1)}, bf16[512,256]{0,1:T(8,128)(2,1)}, u32[]{:S(2)}, u32[]{:S(2)}) collective-permute-start(bf16[512,256]{0,1:T(8,128)(2,1)} %get-tuple-element.145), channel_id=1, source_target_pairs={{0,4},{2,6},{4,0},{6,2},{1,5},{3,7},{5,1},{7,3},{8,12},{10,14},{12... | collective-permute-start | bytes 786440 | tf_op jit(solution)/shard_map/ppermute | solution.py:301
  441.4 14.7 %collective-permute-start.44 = (bf16[512,256]{0,1:T(8,128)(2,1)}, bf16[512,256]{0,1:T(8,128)(2,1)}, u32[]{:S(2)}, u32[]{:S(2)}) collective-permute-start(bf16[512,256]{0,1:T(8,128)(2,1)} %get-tuple-element.144), channel_id=1, source_target_pairs={{0,6},{2,4},{4,2},{6,0},{1,7},{3,5},{5,3},{7,1},{8,14},{10,12},{12... | collective-permute-start | bytes 786440 | tf_op jit(solution)/shard_map/ppermute | solution.py:301
  456.1 13.4 %collective-permute-start.65 = (bf16[512,256]{1,0:T(8,128)(2,1)}, bf16[512,256]{1,0:T(8,128)(2,1)}, u32[]{:S(2)}, u32[]{:S(2)}) collective-permute-start(bf16[512,256]{1,0:T(8,128)(2,1)} %convolution_convert_fusion.15), channel_id=1, source_target_pairs={{0,2},{2,0},{4,6},{6,4},{1,3},{3,1},{5,7},{7,5},{8,10},{10,8},{12,... | collective-permute-start | bytes 786440 | tf_op jit(solution)/shard_map/ppermute | solution.py:301
  457.9 15.6 %collective-permute-start.46 = (bf16[256,1536]{1,0:T(8,128)(2,1)}, bf16[256,1536]{1,0:T(8,128)(2,1)}, u32[]{:S(2)}, u32[]{:S(2)}) collective-permute-start(bf16[256,1536]{1,0:T(8,128)(2,1)} %convolution_convert_fusion.10), channel_id=1, source_target_pairs={{0,2},{2,0},{4,6},{6,4},{1,3},{3,1},{5,7},{7,5},{8,10},{10,8},{12,... | collective-permute-start | bytes 2359304 | tf_op jit(solution)/shard_map/ppermute | solution.py:301
  469.5 18.8 %collective-permute-start.88 = (bf16[2048,256]{1,0:T(8,128)(2,1)}, bf16[2048,256]{1,0:T(8,128)(2,1)S(1)}, u32[]{:S(2)}, u32[]{:S(2)}) collective-permute-start(bf16[2048,256]{1,0:T(8,128)(2,1)} %convolution_convert_fusion), channel_id=1, source_target_pairs={{0,2},{2,0},{4,6},{6,4},{1,3},{3,1},{5,7},{7,5},{8,10},{10,8},{12,... | collective-permute-start | bytes 3145736 | tf_op jit(solution)/shard_map/ppermute | solution.py:301
  478.3 58.8 %collective-permute-start.87 = (bf16[2048,256]{1,0:T(8,128)(2,1)S(1)}, bf16[2048,256]{1,0:T(8,128)(2,1)S(1)}, u32[]{:S(2)}, u32[]{:S(2)}) collective-permute-start(bf16[2048,256]{1,0:T(8,128)(2,1)S(1)} %copy-done.111), channel_id=1, source_target_pairs={{0,2},{2,0},{4,6},{6,4},{1,3},{3,1},{5,7},{7,5},{8,10},{10,8},{12,... | collective-permute-start | bytes 3145736 | tf_op jit(solution)/shard_map/ppermute | solution.py:301
  482.2 16.6 %collective-permute-start.75 = (bf16[256,2048]{1,0:T(8,128)(2,1)S(1)}, bf16[256,2048]{1,0:T(8,128)(2,1)S(1)}, u32[]{:S(2)}, u32[]{:S(2)}) collective-permute-start(bf16[256,2048]{1,0:T(8,128)(2,1)S(1)} %copy-done.76), channel_id=1, source_target_pairs={{0,2},{2,0},{4,6},{6,4},{1,3},{3,1},{5,7},{7,5},{8,10},{10,8},{12,... | collective-permute-start | bytes 3145736 | tf_op jit(solution)/shard_map/ppermute | solution.py:301
  485.1 35.1 %collective-permute-start.78 = (bf16[256,2048]{1,0:T(8,128)(2,1)S(1)}, bf16[256,2048]{1,0:T(8,128)(2,1)S(1)}, u32[]{:S(2)}, u32[]{:S(2)}) collective-permute-start(bf16[256,2048]{1,0:T(8,128)(2,1)S(1)} %copy-done.75), channel_id=1, source_target_pairs={{0,2},{2,0},{4,6},{6,4},{1,3},{3,1},{5,7},{7,5},{8,10},{10,8},{12,... | collective-permute-start | bytes 3145736 | tf_op jit(solution)/shard_map/ppermute | solution.py:301
  485.3 15.3 %collective-permute-start.48 = (bf16[256,1536]{1,0:T(8,128)(2,1)S(1)}, bf16[256,1536]{1,0:T(8,128)(2,1)S(1)}, u32[]{:S(2)}, u32[]{:S(2)}) collective-permute-start(bf16[256,1536]{1,0:T(8,128)(2,1)S(1)} %copy-done.94), channel_id=1, source_target_pairs={{0,2},{2,0},{4,6},{6,4},{1,3},{3,1},{5,7},{7,5},{8,10},{10,8},{12,... | collective-permute-start | bytes 2359304 | tf_op jit(solution)/shard_map/ppermute | solution.py:301
  497.8 20.5 %collective-permute-start.50 = (bf16[256,1536]{1,0:T(8,128)(2,1)S(1)}, bf16[256,1536]{1,0:T(8,128)(2,1)S(1)}, u32[]{:S(2)}, u32[]{:S(2)}) collective-permute-start(bf16[256,1536]{1,0:T(8,128)(2,1)S(1)} %fusion.44), channel_id=1, source_target_pairs={{0,1},{1,0},{2,3},{3,2},{4,5},{5,4},{6,7},{7,6},{8,9},{9,8},{10,11... | collective-permute-start | bytes 2359304 | tf_op jit(solution)/shard_map/ppermute | solution.py:305
  500.4 29.4 %collective-permute-start.45 = (bf16[256,1536]{1,0:T(8,128)(2,1)S(1)}, bf16[256,1536]{1,0:T(8,128)(2,1)S(1)}, u32[]{:S(2)}, u32[]{:S(2)}) collective-permute-start(bf16[256,1536]{1,0:T(8,128)(2,1)S(1)} %copy-done.93), channel_id=1, source_target_pairs={{0,2},{2,0},{4,6},{6,4},{1,3},{3,1},{5,7},{7,5},{8,10},{10,8},{12,... | collective-permute-start | bytes 2359304 | tf_op jit(solution)/shard_map/ppermute | solution.py:301
  500.6 34.5 %collective-permute-start.47 = (bf16[256,1536]{1,0:T(8,128)(2,1)S(1)}, bf16[256,1536]{1,0:T(8,128)(2,1)S(1)}, u32[]{:S(2)}, u32[]{:S(2)}) collective-permute-start(bf16[256,1536]{1,0:T(8,128)(2,1)S(1)} %add_convert_fusion.16), channel_id=1, source_target_pairs={{0,1},{1,0},{2,3},{3,2},{4,5},{5,4},{6,7},{7,6},{8,9},{9,8},{10,11... | collective-permute-start | bytes 2359304 | tf_op jit(solution)/shard_map/ppermute | solution.py:305
  520.2 15.9 %collective-permute-start.51 = (bf16[256,1536]{1,0:T(8,128)(2,1)S(1)}, bf16[256,1536]{1,0:T(8,128)(2,1)S(1)}, u32[]{:S(2)}, u32[]{:S(2)}) collective-permute-start(bf16[256,1536]{1,0:T(8,128)(2,1)S(1)} %fusion.43), channel_id=1, source_target_pairs={{0,4},{2,6},{4,0},{6,2},{1,5},{3,7},{5,1},{7,3},{8,12},{10,14},{12... | collective-permute-start | bytes 2359304 | tf_op jit(solution)/shard_map/ppermute | solution.py:301
  526.5 29.2 %collective-permute-start.89 = (bf16[2048,256]{1,0:T(8,128)(2,1)S(1)}, bf16[2048,256]{1,0:T(8,128)(2,1)S(1)}, u32[]{:S(2)}, u32[]{:S(2)}) collective-permute-start(bf16[2048,256]{1,0:T(8,128)(2,1)S(1)} %add_convert_fusion.4), channel_id=1, source_target_pairs={{0,1},{1,0},{2,3},{3,2},{4,5},{5,4},{6,7},{7,6},{8,9},{9,8},{10,11... | collective-permute-start | bytes 3145736 | tf_op jit(solution)/shard_map/ppermute | solution.py:305
  529.8 32.8 %collective-permute-start.84 = (bf16[2048,256]{1,0:T(8,128)(2,1)S(1)}, bf16[2048,256]{1,0:T(8,128)(2,1)S(1)}, u32[]{:S(2)}, u32[]{:S(2)}) collective-permute-start(bf16[2048,256]{1,0:T(8,128)(2,1)S(1)} %copy-done.110), channel_id=1, source_target_pairs={{0,2},{2,0},{4,6},{6,4},{1,3},{3,1},{5,7},{7,5},{8,10},{10,8},{12,... | collective-permute-start | bytes 3145736 | tf_op jit(solution)/shard_map/ppermute | solution.py:301
  535.1 25.4 %collective-permute-start.77 = (bf16[256,2048]{1,0:T(8,128)(2,1)S(1)}, bf16[256,2048]{1,0:T(8,128)(2,1)S(1)}, u32[]{:S(2)}, u32[]{:S(2)}) collective-permute-start(bf16[256,2048]{1,0:T(8,128)(2,1)S(1)} %copy-done.74), channel_id=1, source_target_pairs={{0,2},{2,0},{4,6},{6,4},{1,3},{3,1},{5,7},{7,5},{8,10},{10,8},{12,... | collective-permute-start | bytes 3145736 | tf_op jit(solution)/shard_map/ppermute | solution.py:301
  536.1 25.4 %collective-permute-start.79 = (bf16[256,2048]{1,0:T(8,128)(2,1)S(1)}, bf16[256,2048]{1,0:T(8,128)(2,1)S(1)}, u32[]{:S(2)}, u32[]{:S(2)}) collective-permute-start(bf16[256,2048]{1,0:T(8,128)(2,1)S(1)} %add_convert_fusion.10), channel_id=1, source_target_pairs={{0,4},{2,6},{4,0},{6,2},{1,5},{3,7},{5,1},{7,3},{8,12},{10,14},{12... | collective-permute-start | bytes 3145736 | tf_op jit(solution)/shard_map/ppermute | solution.py:301
  537.1 54.9 %collective-permute-start.74 = (bf16[256,2048]{1,0:T(8,128)(2,1)S(1)}, bf16[256,2048]{1,0:T(8,128)(2,1)S(1)}, u32[]{:S(2)}, u32[]{:S(2)}) collective-permute-start(bf16[256,2048]{1,0:T(8,128)(2,1)S(1)} %copy-done.73), channel_id=1, source_target_pairs={{0,2},{2,0},{4,6},{6,4},{1,3},{3,1},{5,7},{7,5},{8,10},{10,8},{12,... | collective-permute-start | bytes 3145736 | tf_op jit(solution)/shard_map/ppermute | solution.py:301
  555.7 19.6 %collective-permute-start.52 = (bf16[256,1536]{1,0:T(8,128)(2,1)S(1)}, bf16[256,1536]{1,0:T(8,128)(2,1)S(1)}, u32[]{:S(2)}, u32[]{:S(2)}) collective-permute-start(bf16[256,1536]{1,0:T(8,128)(2,1)S(1)} %add_convert_fusion.15), channel_id=1, source_target_pairs={{0,8},{24,16},{1,9},{25,17},{2,10},{26,18},{3,11},{27,19},{4,12},{... | collective-permute-start | bytes 2359304 | tf_op jit(solution)/shard_map/ppermute | solution.py:353
  560.5 26.2 %collective-permute-start.86 = (bf16[2048,256]{1,0:T(8,128)(2,1)S(1)}, bf16[2048,256]{1,0:T(8,128)(2,1)S(1)}, u32[]{:S(2)}, u32[]{:S(2)}) collective-permute-start(bf16[2048,256]{1,0:T(8,128)(2,1)S(1)} %add_convert_fusion.5), channel_id=1, source_target_pairs={{0,1},{1,0},{2,3},{3,2},{4,5},{5,4},{6,7},{7,6},{8,9},{9,8},{10,11... | collective-permute-start | bytes 3145736 | tf_op jit(solution)/shard_map/ppermute | solution.py:305
  561.6 26.1 %collective-permute-start.90 = (bf16[2048,256]{1,0:T(8,128)(2,1)S(1)}, bf16[2048,256]{1,0:T(8,128)(2,1)S(1)}, u32[]{:S(2)}, u32[]{:S(2)}) collective-permute-start(bf16[2048,256]{1,0:T(8,128)(2,1)S(1)} %add_convert_fusion.3), channel_id=1, source_target_pairs={{0,4},{2,6},{4,0},{6,2},{1,5},{3,7},{5,1},{7,3},{8,12},{10,14},{12... | collective-permute-start | bytes 3145736 | tf_op jit(solution)/shard_map/ppermute | solution.py:301
  562.7 44.1 %collective-permute-start.76 = (bf16[256,2048]{1,0:T(8,128)(2,1)S(1)}, bf16[256,2048]{1,0:T(8,128)(2,1)S(1)}, u32[]{:S(2)}, u32[]{:S(2)}) collective-permute-start(bf16[256,2048]{1,0:T(8,128)(2,1)S(1)} %add_convert_fusion.11), channel_id=1, source_target_pairs={{0,4},{2,6},{4,0},{6,2},{1,5},{3,7},{5,1},{7,3},{8,12},{10,14},{12... | collective-permute-start | bytes 3145736 | tf_op jit(solution)/shard_map/ppermute | solution.py:301
  575.3 31.5 %collective-permute-start.80 = (bf16[256,2048]{1,0:T(8,128)(2,1)S(1)}, bf16[256,2048]{1,0:T(8,128)(2,1)S(1)}, u32[]{:S(2)}, u32[]{:S(2)}) collective-permute-start(bf16[256,2048]{1,0:T(8,128)(2,1)S(1)} %add_convert_fusion.9), channel_id=1, source_target_pairs={{0,1},{1,0},{2,3},{3,2},{4,5},{5,4},{6,7},{7,6},{8,9},{9,8},{10,11... | collective-permute-start | bytes 3145736 | tf_op jit(solution)/shard_map/ppermute | solution.py:305
  586.7 25.2 %collective-permute-start.53 = (bf16[256,1536]{1,0:T(8,128)(2,1)S(1)}, bf16[256,1536]{1,0:T(8,128)(2,1)S(1)}, u32[]{:S(2)}, u32[]{:S(2)}) collective-permute-start(bf16[256,1536]{1,0:T(8,128)(2,1)S(1)} %add_convert_fusion.14), channel_id=1, source_target_pairs={{8,16},{16,8},{9,17},{17,9},{10,18},{18,10},{11,19},{19,11},{12,20... | collective-permute-start | bytes 2359304 | tf_op jit(solution)/shard_map/ppermute | solution.py:355
  588.1 25.2 %collective-permute-start.91 = (bf16[2048,256]{1,0:T(8,128)(2,1)S(1)}, bf16[2048,256]{1,0:T(8,128)(2,1)S(1)}, u32[]{:S(2)}, u32[]{:S(2)}) collective-permute-start(bf16[2048,256]{1,0:T(8,128)(2,1)S(1)} %add_convert_fusion.2), channel_id=1, source_target_pairs={{0,8},{24,16},{1,9},{25,17},{2,10},{26,18},{3,11},{27,19},{4,12},{... | collective-permute-start | bytes 3145736 | tf_op jit(solution)/shard_map/ppermute | solution.py:353
  607.5 24.5 %collective-permute-start.81 = (bf16[256,2048]{1,0:T(8,128)(2,1)S(1)}, bf16[256,2048]{1,0:T(8,128)(2,1)S(1)}, u32[]{:S(2)}, u32[]{:S(2)}) collective-permute-start(bf16[256,2048]{1,0:T(8,128)(2,1)S(1)} %add_convert_fusion.8), channel_id=1, source_target_pairs={{0,8},{24,16},{1,9},{25,17},{2,10},{26,18},{3,11},{27,19},{4,12},{... | collective-permute-start | bytes 3145736 | tf_op jit(solution)/shard_map/ppermute | solution.py:353
  612.1 22.9 %collective-permute-start.54 = (bf16[256,1536]{1,0:T(8,128)(2,1)S(1)}, bf16[256,1536]{1,0:T(8,128)(2,1)S(1)}, u32[]{:S(2)}, u32[]{:S(2)}) collective-permute-start(bf16[256,1536]{1,0:T(8,128)(2,1)S(1)} %add_convert_fusion.13), channel_id=1, source_target_pairs={{8,0},{16,24},{9,1},{17,25},{10,2},{18,26},{11,3},{19,27},{12,4},{... | collective-permute-start | bytes 2359304 | tf_op jit(solution)/shard_map/ppermute | solution.py:357
  614.7 25.5 %collective-permute-start.92 = (bf16[2048,256]{1,0:T(8,128)(2,1)}, bf16[2048,256]{1,0:T(8,128)(2,1)}, u32[]{:S(2)}, u32[]{:S(2)}) collective-permute-start(bf16[2048,256]{1,0:T(8,128)(2,1)} %add_convert_fusion.1), channel_id=1, source_target_pairs={{8,16},{16,8},{9,17},{17,9},{10,18},{18,10},{11,19},{19,11},{12,20... | collective-permute-start | bytes 3145736 | tf_op jit(solution)/shard_map/ppermute | solution.py:355
  633.3 24.6 %collective-permute-start.82 = (bf16[256,2048]{1,0:T(8,128)(2,1)}, bf16[256,2048]{1,0:T(8,128)(2,1)}, u32[]{:S(2)}, u32[]{:S(2)}) collective-permute-start(bf16[256,2048]{1,0:T(8,128)(2,1)} %add_convert_fusion.7), channel_id=1, source_target_pairs={{8,16},{16,8},{9,17},{17,9},{10,18},{18,10},{11,19},{19,11},{12,20... | collective-permute-start | bytes 3145736 | tf_op jit(solution)/shard_map/ppermute | solution.py:355
  642.9 30.0 %collective-permute-start.93 = (bf16[2048,256]{1,0:T(8,128)(2,1)}, bf16[2048,256]{1,0:T(8,128)(2,1)}, u32[]{:S(2)}, u32[]{:S(2)}) collective-permute-start(bf16[2048,256]{1,0:T(8,128)(2,1)} %add_convert_fusion), channel_id=1, source_target_pairs={{8,0},{16,24},{9,1},{17,25},{10,2},{18,26},{11,3},{19,27},{12,4},{... | collective-permute-start | bytes 3145736 | tf_op jit(solution)/shard_map/ppermute | solution.py:357
  659.8 31.2 %collective-permute-start.83 = (bf16[256,2048]{1,0:T(8,128)(2,1)S(1)}, bf16[256,2048]{1,0:T(8,128)(2,1)S(1)}, u32[]{:S(2)}, u32[]{:S(2)}) collective-permute-start(bf16[256,2048]{1,0:T(8,128)(2,1)S(1)} %add_convert_fusion.6), channel_id=1, source_target_pairs={{8,0},{16,24},{9,1},{17,25},{10,2},{18,26},{11,3},{19,27},{12,4},{... | collective-permute-start | bytes 3145736 | tf_op jit(solution)/shard_map/ppermute | solution.py:357
  (146 other events, 1675.7 us)
